TPU v7x, 256 devices: a whole 4x4x8 slice. The times are simulated.
256 devices in a mesh: freq: 8 (over y, z_hi), dom: 32 (over x, z_lo, core).
Axes of the slice: x: 4, y: 4, z: 8 (z_hi: 2, z_lo: 4; z = z_hi * 4 + z_lo), core: 2. Of those that a mesh axis runs over, the one named last changes fastest.
Arguments:
- fwd_source: float32 [16, 4, 1024, 128], P('freq', None, 'dom'), may hold values from -6 to 6
- adj_source: float32 [16, 4, 1024, 128], P('freq', None, 'dom'), may hold values from -6 to 6
- curl_blocks: float32 [1024, 4, 128, 128], P('dom')
- block_links: int32 [1024, 4], P('dom'), may hold values from 0 to 95, as said below
- tile_lists: int32 [128, 16], P('dom'), may hold values from 0 to 31, as said below
- edge_mass: float32 [1024, 128], P('dom'), may hold values from 0.5 to 1.5
- omega: float32 [16], P('freq'), may hold values from 0.1 to 1
- cell_edges: int32 [12, 32768], P(None, 'dom'), may hold values from 0 to 4095
- log_cond: float32 [32768], P('dom'), may hold values from -6 to 6
Outputs:
- fwd_field: float32 [16, 4, 1024, 128], P('freq', None, 'dom')
- adj_field: float32 [16, 4, 1024, 128], P('freq', None, 'dom')
- model_next: float32 [32768], P('dom')
Inputs may be any that keep to these rules, and one draw needn't show every extreme that they name: `block_links`: entry 0 of each block row is the row's own local block; the others index the partition's extended field, local blocks first, then the tiles received in round 0, 1 and so on; every received tile is referenced by some row of the partition. `tile_lists`: the 16 blocks of one row are distinct local blocks.
All inputs are finite; a program needn't handle non-finite values.
Results may differ from a plain program's by a relative error of at most 0.0001.
Values sent between devices are 32-bit elements; how exact they have to be, the bound alone decides.
No kernel may reach another device: no remote copies, remote signals or barrier semaphores. Data moves between devices by JAX's collectives and lax.ppermute only.
A program may use at most 64 MiB of HBM per device.

v0:
```python
import jax
import jax.numpy as jnp
from jax import lax
from jax.sharding import PartitionSpec as P

ITERS = 3


def swapped(value, axis, distance):
    mask = 2**distance
    pairs = [(source, source ^ mask) for source in range(lax.axis_size(axis))]
    return lax.ppermute(value, axis, pairs)


def operate(field, curl_blocks, block_links, tile_lists, weight, trade):
    parts = [field]
    for bit in range(tile_lists.shape[0]):
        outgoing = jnp.take(field, tile_lists[bit], axis=0)
        parts.append(trade(outgoing, bit))
    extended = jnp.concatenate(parts, axis=0)
    shape = field.shape
    gathered = jnp.take(extended, block_links.reshape(-1), axis=0)
    gathered = gathered.reshape(block_links.shape + shape[1:])
    curl = jnp.einsum("blij,blmj->bmi", curl_blocks, gathered, precision=lax.Precision.HIGHEST)
    count = weight.shape[2]
    curl = curl.reshape(shape[0], -1, count, 2, 2, shape[2])
    split = field.reshape(shape[0], -1, count, 2, 2, shape[2])
    real_part = curl[:, :, :, :, 0] - weight * split[:, :, :, :, 1]
    imag_part = curl[:, :, :, :, 1] + weight * split[:, :, :, :, 0]
    return jnp.stack([real_part, imag_part], axis=4).reshape(shape)


def chebyshev(source, curl_blocks, block_links, tile_lists, weight, trade):
    theta = 1.0
    delta = 0.7
    sone = theta / delta
    rho = 1.0 / sone
    solution = jnp.zeros_like(source)
    resid = source
    direction = source / theta
    for step in range(ITERS):
        solution = solution + direction
        if step + 1 < ITERS:
            resid = resid - operate(direction, curl_blocks, block_links, tile_lists, weight, trade)
            rho_new = 1.0 / (2.0 * sone - rho)
            direction = rho_new * rho * direction + 2.0 * rho_new / delta * resid
            rho = rho_new
    return solution


def to_rows(fields):
    shape = fields.shape
    moved = jnp.transpose(fields, (3, 0, 1, 2, 4))
    return moved.reshape(shape[3], shape[0] * shape[1] * shape[2], shape[4])


def from_rows(rows, systems, count):
    shaped = rows.reshape(rows.shape[0], systems, count, 4, rows.shape[2])
    return jnp.transpose(shaped, (1, 2, 3, 0, 4))


def local(
    fwd_source,
    adj_source,
    curl_blocks,
    block_links,
    tile_lists,
    edge_mass,
    omega,
    cell_edges,
    log_cond,
):
    count = fwd_source.shape[0]
    weight = (edge_mass[:, None, :] * omega[None, :, None])[:, None, :, None, :]

    def trade_one(outgoing, bit):
        return swapped(outgoing, "dom", bit)

    fwd_rows = chebyshev(
        to_rows(fwd_source[None]), curl_blocks, block_links, tile_lists, weight, trade_one
    )
    adj_rows = chebyshev(
        to_rows(adj_source[None]), curl_blocks, block_links, tile_lists, weight, trade_one
    )
    efield = from_rows(fwd_rows, 1, count)[0]
    lfield = from_rows(adj_rows, 1, count)[0]
    edges = efield.shape[2] * efield.shape[3]
    esplit = efield.reshape(count, 2, 2, edges)
    lsplit = lfield.reshape(count, 2, 2, edges)
    prod = esplit[:, :, 0] * lsplit[:, :, 1] + esplit[:, :, 1] * lsplit[:, :, 0]
    edge_term = jnp.sum(omega[:, None, None] * prod, axis=(0, 1))
    picked = jnp.take(edge_term, cell_edges.reshape(-1), axis=0).reshape(cell_edges.shape)
    scale = 1.0 / jnp.sqrt(24.0 * count * lax.axis_size("freq"))
    partial_grad = jnp.sum(picked, axis=0) * scale
    grad = lax.psum(partial_grad, "freq")
    model_next = log_cond - 0.5 * grad / jnp.sqrt(grad * grad + 1.0)
    return (efield, lfield, model_next)


def solution(mesh):
    in_specs = (
        P("freq", None, "dom", None),
        P("freq", None, "dom", None),
        P("dom", None, None, None),
        P("dom", None),
        P("dom", None),
        P("dom", None),
        P("freq"),
        P(None, "dom"),
        P("dom"),
    )
    out_specs = (P("freq", None, "dom", None), P("freq", None, "dom", None), P("dom"))
    return jax.shard_map(local, mesh=mesh, in_specs=in_specs, out_specs=out_specs, check_vma=False)
```

profile of v0, /device:TPU:4, one launch (start us, length us, event | category | flops | bytes accessed | tf_op | source)
XLA Modules:
  0.0 182.5 jit_solution(15824569040240050575)
XLA Ops:
  0.6 0.8 compare_and_fusion.1
  1.5 1.0 copy.47
  2.5 1.0 copy.51
  6.1 2.0 %collective-permute-start.1 = (f32[16,8,128]{2,1,0:T(8,128)S(1)}, f32[16,8,128]{2,1,0:T(8,128)S(1)}, u32[]{:S(2)}, u32[]{:S(2)}) collective-permute-start(f32[16,8,128]{2,1,0:T(8,128)S(1)} %get-tuple-element.60), channel_id=1, source_target_pairs={{0,2},{1,3},{2,0},{3,1},{4,6},{5,7},{6,4},{7,5},{8,10},{9,11},{10,... | collective-permute-start | bytes 196616 | tf_op jit(solution)/shard_map/ppermute | solution.py:12
  9.3 3.4 %collective-permute-start.2 = (f32[16,8,128]{2,1,0:T(8,128)S(1)}, f32[16,8,128]{2,1,0:T(8,128)S(1)}, u32[]{:S(2)}, u32[]{:S(2)}) collective-permute-start(f32[16,8,128]{2,1,0:T(8,128)S(1)} %get-tuple-element.58), channel_id=1, source_target_pairs={{0,4},{1,5},{2,6},{3,7},{4,0},{5,1},{6,2},{7,3},{8,12},{9,13},{10,... | collective-permute-start | bytes 196616 | tf_op jit(solution)/shard_map/ppermute | solution.py:12
  13.9 1.3 collective-permute-start.3
  15.2 0.8 copy.46
  16.1 0.9 copy.60
  17.1 0.8 broadcast_multiply_fusion
  18.4 1.1 collective-permute-start.11
  20.3 3.4 %collective-permute-done.9 = f32[16,8,128]{2,1,0:T(8,128)S(1)} collective-permute-done((f32[16,8,128]{2,1,0:T(8,128)S(1)}, f32[16,8,128]{2,1,0:T(8,128)S(1)}, u32[]{:S(2)}, u32[]{:S(2)}) %collective-permute-start.9) | collective-permute-done | bytes 65568 | tf_op jit(solution)/shard_map/ppermute | solution.py:12
  23.7 1.3 collective-permute-done.10
  25.0 0.8 gather_fusion.15
  26.0 9.3 %convolution_bitcast_fusion.3 = f32[32,8,128]{2,1,0:T(8,128)S(1)} fusion(f32[32,4,8,128]{3,2,1,0:T(8,128)S(1)} %bitcast.106, f32[32,4,128,128]{3,2,1,0:T(8,128)} %param.15), kind=kOutput, calls=%fused_computation.24 | convolution fusion | flops 201326592 | bytes 9043968 | tf_op jit(solution)/shard_map/blij,blmj->bmi/dot_general | solution.py:24
  35.4 9.3 %convolution_bitcast_fusion.1 = f32[32,8,128]{2,1,0:T(8,128)S(1)} fusion(f32[32,4,8,128]{3,2,1,0:T(8,128)S(1)} %bitcast.104, f32[32,4,128,128]{3,2,1,0:T(8,128)} %param.15), kind=kOutput, calls=%fused_computation.22 | convolution fusion | flops 201326592 | bytes 9043968 | tf_op jit(solution)/shard_map/blij,blmj->bmi/dot_general | solution.py:24
  50.4 2.3 %collective-permute-start.6 = (f32[16,8,128]{2,1,0:T(8,128)S(1)}, f32[16,8,128]{2,1,0:T(8,128)S(1)}, u32[]{:S(2)}, u32[]{:S(2)}) collective-permute-start(f32[16,8,128]{2,1,0:T(8,128)S(1)} %get-tuple-element.48), channel_id=1, source_target_pairs={{0,4},{1,5},{2,6},{3,7},{4,0},{5,1},{6,2},{7,3},{8,12},{9,13},{10,... | collective-permute-start | bytes 196616 | tf_op jit(solution)/shard_map/ppermute | solution.py:12
  52.8 0.9 collective-permute-start.7
  53.8 1.2 collective-permute-start.15
  55.7 1.8 collective-permute-start.13
  59.0 1.7 collective-permute-done.13
  61.8 9.3 %convolution_bitcast_fusion.2 = f32[32,8,128]{2,1,0:T(8,128)S(1)} fusion(f32[32,4,8,128]{3,2,1,0:T(8,128)S(1)} %bitcast.105, f32[32,4,128,128]{3,2,1,0:T(8,128)} %param.15), kind=kOutput, calls=%fused_computation.23 | convolution fusion | flops 201326592 | bytes 9043968 | tf_op jit(solution)/shard_map/blij,blmj->bmi/dot_general | solution.py:24
  71.1 9.3 %convolution_bitcast_fusion = f32[32,8,128]{2,1,0:T(8,128)S(1)} fusion(f32[32,4,8,128]{3,2,1,0:T(8,128)S(1)} %bitcast.103, f32[32,4,128,128]{3,2,1,0:T(8,128)} %param.15), kind=kOutput, calls=%fused_computation.21 | convolution fusion | flops 201326592 | bytes 9043968 | tf_op jit(solution)/shard_map/blij,blmj->bmi/dot_general | solution.py:24
  82.3 68.0 %gather_fusion = f32[12288]{0:T(1024)S(1)} fusion(f32[4096]{0:T(1024)S(1)} %fusion.13, s32[12288]{0:T(1024)S(1)} %broadcast_clamp_fusion), kind=kCustom, calls=%fused_computation.20 | custom fusion | bytes 147456 | tf_op jit(solution)/shard_map/jit(_take)/gather | solution.py:92
  150.5 31.5 %psum.7 = f32[1024]{0:T(1024)S(1)} all-reduce(f32[1024]{0:T(1024)S(1)} %broadcast_multiply_fusion.1), channel_id=1, replica_groups=mesh['freq'=8,'dom'=32] {'freq'}, use_global_device_ids=true, to_apply=%region_2.5 | all-reduce | flops 1024 | bytes 8192 | tf_op jit(solution)/shard_map/psum | solution.py:95
  (109 shorter events, 18.3 us)
Async XLA Ops:
  4.7 13.2 %collective-permute-start = (f32[16,8,128]{2,1,0:T(8,128)S(1)}, f32[16,8,128]{2,1,0:T(8,128)S(1)}, u32[]{:S(2)}, u32[]{:S(2)}) collective-permute-start(f32[16,8,128]{2,1,0:T(8,128)S(1)} %get-tuple-element.62), channel_id=1, source_target_pairs={{0,1},{1,0},{2,3},{3,2},{4,5},{5,4},{6,7},{7,6},{8,9},{9,8},{10,11... | collective-permute-start | bytes 196616 | tf_op jit(solution)/shard_map/ppermute | solution.py:12
  6.1 12.1 %collective-permute-start.1 = (f32[16,8,128]{2,1,0:T(8,128)S(1)}, f32[16,8,128]{2,1,0:T(8,128)S(1)}, u32[]{:S(2)}, u32[]{:S(2)}) collective-permute-start(f32[16,8,128]{2,1,0:T(8,128)S(1)} %get-tuple-element.60), channel_id=1, source_target_pairs={{0,2},{1,3},{2,0},{3,1},{4,6},{5,7},{6,4},{7,5},{8,10},{9,11},{10,... | collective-permute-start | bytes 196616 | tf_op jit(solution)/shard_map/ppermute | solution.py:12
  9.3 9.1 %collective-permute-start.2 = (f32[16,8,128]{2,1,0:T(8,128)S(1)}, f32[16,8,128]{2,1,0:T(8,128)S(1)}, u32[]{:S(2)}, u32[]{:S(2)}) collective-permute-start(f32[16,8,128]{2,1,0:T(8,128)S(1)} %get-tuple-element.58), channel_id=1, source_target_pairs={{0,4},{1,5},{2,6},{3,7},{4,0},{5,1},{6,2},{7,3},{8,12},{9,13},{10,... | collective-permute-start | bytes 196616 | tf_op jit(solution)/shard_map/ppermute | solution.py:12
  13.9 5.6 %collective-permute-start.3 = (f32[16,8,128]{2,1,0:T(8,128)S(1)}, f32[16,8,128]{2,1,0:T(8,128)S(1)}, u32[]{:S(2)}, u32[]{:S(2)}) collective-permute-start(f32[16,8,128]{2,1,0:T(8,128)S(1)} %get-tuple-element.56), channel_id=1, source_target_pairs={{0,8},{1,9},{2,10},{3,11},{4,12},{5,13},{6,14},{7,15},{8,0},{9,1},... | collective-permute-start | bytes 196616 | tf_op jit(solution)/shard_map/ppermute | solution.py:12
  15.2 5.1 %collective-permute-start.8 = (f32[16,8,128]{2,1,0:T(8,128)S(1)}, f32[16,8,128]{2,1,0:T(8,128)S(1)}, u32[]{:S(2)}, u32[]{:S(2)}) collective-permute-start(f32[16,8,128]{2,1,0:T(8,128)S(1)} %get-tuple-element.61), channel_id=1, source_target_pairs={{0,1},{1,0},{2,3},{3,2},{4,5},{5,4},{6,7},{7,6},{8,9},{9,8},{10,11... | collective-permute-start | bytes 196616 | tf_op jit(solution)/shard_map/ppermute | solution.py:12
  17.9 5.8 %collective-permute-start.9 = (f32[16,8,128]{2,1,0:T(8,128)S(1)}, f32[16,8,128]{2,1,0:T(8,128)S(1)}, u32[]{:S(2)}, u32[]{:S(2)}) collective-permute-start(f32[16,8,128]{2,1,0:T(8,128)S(1)} %get-tuple-element.59), channel_id=1, source_target_pairs={{0,2},{1,3},{2,0},{3,1},{4,6},{5,7},{6,4},{7,5},{8,10},{9,11},{10,... | collective-permute-start | bytes 196616 | tf_op jit(solution)/shard_map/ppermute | solution.py:12
  18.1 6.9 %collective-permute-start.10 = (f32[16,8,128]{2,1,0:T(8,128)S(1)}, f32[16,8,128]{2,1,0:T(8,128)S(1)}, u32[]{:S(2)}, u32[]{:S(2)}) collective-permute-start(f32[16,8,128]{2,1,0:T(8,128)S(1)} %get-tuple-element.57), channel_id=1, source_target_pairs={{0,4},{1,5},{2,6},{3,7},{4,0},{5,1},{6,2},{7,3},{8,12},{9,13},{10,... | collective-permute-start | bytes 196616 | tf_op jit(solution)/shard_map/ppermute | solution.py:12
  18.4 6.6 %collective-permute-start.11 = (f32[16,8,128]{2,1,0:T(8,128)S(1)}, f32[16,8,128]{2,1,0:T(8,128)S(1)}, u32[]{:S(2)}, u32[]{:S(2)}) collective-permute-start(f32[16,8,128]{2,1,0:T(8,128)S(1)} %get-tuple-element.55), channel_id=1, source_target_pairs={{0,8},{1,9},{2,10},{3,11},{4,12},{5,13},{6,14},{7,15},{8,0},{9,1},... | collective-permute-start | bytes 196616 | tf_op jit(solution)/shard_map/ppermute | solution.py:12
  26.0 18.7 %copy-start = (f32[2,4,32,128]{3,2,1,0:T(8,128)S(1)}, f32[2,4,32,128]{3,2,1,0:T(8,128)}, u32[]{:S(2)}) copy-start(f32[2,4,32,128]{3,2,1,0:T(8,128)} %param.14) | copy-start | bytes 393220
  26.0 18.7 %copy-start.1 = (f32[2,4,32,128]{3,2,1,0:T(8,128)S(1)}, f32[2,4,32,128]{3,2,1,0:T(8,128)}, u32[]{:S(2)}) copy-start(f32[2,4,32,128]{3,2,1,0:T(8,128)} %param.13) | copy-start | bytes 393220
  49.7 5.2 %collective-permute-start.4 = (f32[16,8,128]{2,1,0:T(8,128)S(1)}, f32[16,8,128]{2,1,0:T(8,128)S(1)}, u32[]{:S(2)}, u32[]{:S(2)}) collective-permute-start(f32[16,8,128]{2,1,0:T(8,128)S(1)} %get-tuple-element.52), channel_id=1, source_target_pairs={{0,1},{1,0},{2,3},{3,2},{4,5},{5,4},{6,7},{7,6},{8,9},{9,8},{10,11... | collective-permute-start | bytes 196616 | tf_op jit(solution)/shard_map/ppermute | solution.py:12
  49.9 5.8 %collective-permute-start.5 = (f32[16,8,128]{2,1,0:T(8,128)S(1)}, f32[16,8,128]{2,1,0:T(8,128)S(1)}, u32[]{:S(2)}, u32[]{:S(2)}) collective-permute-start(f32[16,8,128]{2,1,0:T(8,128)S(1)} %get-tuple-element.50), channel_id=1, source_target_pairs={{0,2},{1,3},{2,0},{3,1},{4,6},{5,7},{6,4},{7,5},{8,10},{9,11},{10,... | collective-permute-start | bytes 196616 | tf_op jit(solution)/shard_map/ppermute | solution.py:12
  50.4 7.0 %collective-permute-start.6 = (f32[16,8,128]{2,1,0:T(8,128)S(1)}, f32[16,8,128]{2,1,0:T(8,128)S(1)}, u32[]{:S(2)}, u32[]{:S(2)}) collective-permute-start(f32[16,8,128]{2,1,0:T(8,128)S(1)} %get-tuple-element.48), channel_id=1, source_target_pairs={{0,4},{1,5},{2,6},{3,7},{4,0},{5,1},{6,2},{7,3},{8,12},{9,13},{10,... | collective-permute-start | bytes 196616 | tf_op jit(solution)/shard_map/ppermute | solution.py:12
  52.8 4.9 %collective-permute-start.7 = (f32[16,8,128]{2,1,0:T(8,128)S(1)}, f32[16,8,128]{2,1,0:T(8,128)S(1)}, u32[]{:S(2)}, u32[]{:S(2)}) collective-permute-start(f32[16,8,128]{2,1,0:T(8,128)S(1)} %get-tuple-element.46), channel_id=1, source_target_pairs={{0,8},{1,9},{2,10},{3,11},{4,12},{5,13},{6,14},{7,15},{8,0},{9,1},... | collective-permute-start | bytes 196616 | tf_op jit(solution)/shard_map/ppermute | solution.py:12
  53.8 7.0 %collective-permute-start.15 = (f32[16,8,128]{2,1,0:T(8,128)S(1)}, f32[16,8,128]{2,1,0:T(8,128)S(1)}, u32[]{:S(2)}, u32[]{:S(2)}) collective-permute-start(f32[16,8,128]{2,1,0:T(8,128)S(1)} %get-tuple-element.45), channel_id=1, source_target_pairs={{0,8},{1,9},{2,10},{3,11},{4,12},{5,13},{6,14},{7,15},{8,0},{9,1},... | collective-permute-start | bytes 196616 | tf_op jit(solution)/shard_map/ppermute | solution.py:12
  55.0 5.8 %collective-permute-start.14 = (f32[16,8,128]{2,1,0:T(8,128)S(1)}, f32[16,8,128]{2,1,0:T(8,128)S(1)}, u32[]{:S(2)}, u32[]{:S(2)}) collective-permute-start(f32[16,8,128]{2,1,0:T(8,128)S(1)} %get-tuple-element.47), channel_id=1, source_target_pairs={{0,4},{1,5},{2,6},{3,7},{4,0},{5,1},{6,2},{7,3},{8,12},{9,13},{10,... | collective-permute-start | bytes 196616 | tf_op jit(solution)/shard_map/ppermute | solution.py:12
  55.7 5.1 %collective-permute-start.13 = (f32[16,8,128]{2,1,0:T(8,128)S(1)}, f32[16,8,128]{2,1,0:T(8,128)S(1)}, u32[]{:S(2)}, u32[]{:S(2)}) collective-permute-start(f32[16,8,128]{2,1,0:T(8,128)S(1)} %get-tuple-element.49), channel_id=1, source_target_pairs={{0,2},{1,3},{2,0},{3,1},{4,6},{5,7},{6,4},{7,5},{8,10},{9,11},{10,... | collective-permute-start | bytes 196616 | tf_op jit(solution)/shard_map/ppermute | solution.py:12
  57.4 1.6 collective-permute-start.12
  71.0 11.1 %copy-start.4 = (f32[2]{0:T(128)S(1)}, f32[2]{0:T(128)}, u32[]{:S(2)}) copy-start(f32[2]{0:T(128)} %param.19) | copy-start | bytes 28
  82.3 68.1 %copy-start.2 = (s32[12,1024]{1,0:T(8,128)S(1)}, s32[12,1024]{1,0:T(8,128)}, u32[]{:S(2)}) copy-start(s32[12,1024]{1,0:T(8,128)} %param.20) | copy-start | bytes 147460
  82.3 99.6 %copy-start.3 = (f32[1024]{0:T(1024)S(1)}, f32[1024]{0:T(1024)}, u32[]{:S(2)}) copy-start(f32[1024]{0:T(1024)} %param.21) | copy-start | bytes 12292
where the time goes:
time: 183 us
  local copies, waits for them, and re-layouts  84.3 us (46%)
  matrix products  37 us (20%)
  blocking collectives  31.5 us (17%)
  starting transfers between devices  16 us (9%)
  waiting for transfers between devices  6.85 us (4%)
  other arithmetic  5.52 us (3%)
    gather x2, local copies, waits for them, and re-layouts, local(): jnp.take(edge_term, cell_edges.reshape(-1), axis=0)  68 us
    dot_general x4, matrix products, operate(): jnp.einsum('blij,blmj->bmi', curl_blocks, gathered, precision=lax.Precisi...  37 us
    psum x1, blocking collectives, local(): grad = lax.psum(partial_grad, 'freq')  31.5 us
    ppermute x16, starting transfers between devices, swapped(): return lax.ppermute(value, axis, pairs)  16 us
    gather x16, local copies, waits for them, and re-layouts, operate(): outgoing = jnp.take(field, tile_lists[bit], axis=0)  9.04 us
    ppermute x16, waiting for transfers between devices, swapped(): return lax.ppermute(value, axis, pairs)  6.85 us
  transfers between devices with their start and end apart: 16, of which 4 were waited for; matrix products, arithmetic and copies ran while one was open for 4% of the time, Pallas kernels for 0%

commit v1 on v0

v1 whole, which is shorter than its diff:
```python
import math

import jax
import jax.numpy as jnp
from jax import lax
from jax.experimental import pallas as pl
from jax.experimental.pallas import tpu as pltpu
from jax.sharding import PartitionSpec as P

THETA = 1.0
DELTA = 0.7
SONE = THETA / DELTA
RHO0 = 1.0 / SONE
RHO1 = 1.0 / (2.0 * SONE - RHO0)
RHO2 = 1.0 / (2.0 * SONE - RHO1)
C1, C2 = RHO1 * RHO0, 2.0 * RHO1 / DELTA
C3, C4 = RHO2 * RHO1, 2.0 * RHO2 / DELTA

F32, BF16 = jnp.float32, jnp.bfloat16
VM = pl.BlockSpec(memory_space=pltpu.VMEM)
SM = pl.BlockSpec(memory_space=pltpu.SMEM)
NT = (((1,), (1,)), ((), ()))


def swapped(value, axis, mask):
    pairs = [(source, source ^ mask) for source in range(lax.axis_size(axis))]
    return lax.ppermute(value, axis, pairs)


def near(value):
    return pltpu.with_memory_space_constraint(value, pltpu.VMEM)


def params(mib):
    return pltpu.CompilerParams(vmem_limit_bytes=mib << 20)


def cost(flops, moved):
    return pl.CostEstimate(flops=flops, bytes_accessed=moved, transcendentals=0)


def halves(value):
    high = value.astype(BF16)
    return high, (value - high.astype(F32)).astype(BF16)


def other(value):
    count = value.shape[0]
    even = lax.broadcasted_iota(jnp.int32, value.shape, 0) % 2 == 0
    return jnp.where(even, pltpu.roll(value, count - 1, 0), pltpu.roll(value, 1, 0))


def frequency_rows(omega_ref, rows, lanes):
    row = lax.broadcasted_iota(jnp.int32, (rows, lanes), 0)
    count = omega_ref.shape[0]
    which = (row // 4) % count
    out = jnp.full((rows, lanes), omega_ref[0], F32)
    for f in range(1, count):
        out = jnp.where(which == f, omega_ref[f], out)
    return out, row % 2 == 0


def pick(tiles_ref, field_ref, send_refs):
    for r, send_ref in enumerate(send_refs):
        for t in range(send_ref.shape[0]):
            send_ref[t] = field_ref[tiles_ref[r, t]]


def prepare(tiles_ref, fwd_ref, adj_ref, field_ref, *send_refs):
    blocks, rows, _ = field_ref.shape
    half = rows // 2
    for b in range(blocks):
        field_ref[b, :half] = fwd_ref[pl.ds(b, half, stride=blocks), :]
        field_ref[b, half:] = adj_ref[pl.ds(b, half, stride=blocks), :]
    pick(tiles_ref, field_ref, send_refs)


def split(curl_ref, high_ref, low_ref, buf, sems):
    blocks, links, width, _ = curl_ref.shape
    copies = [
        pltpu.make_async_copy(curl_ref.at[b], buf.at[b], sems.at[b]) for b in range(blocks)
    ]
    for copy in copies:
        copy.start()
    for b in range(blocks):
        copies[b].wait()
        for k in range(links):
            high, low = halves(buf[b, k])
            high_ref[b, :, k * width : (k + 1) * width] = high
            low_ref[b, :, k * width : (k + 1) * width] = low


def extend(field_ref, got_refs, ext):
    blocks, rows, _ = field_ref.shape
    at = 0
    for ref in (field_ref, *got_refs):
        for t in range(ref.shape[0]):
            high, low = halves(ref[t])
            ext[at, :rows] = high
            ext[at, rows:] = low
            at += 1


def curl_row(b, links_ref, high_ref, low_ref, ext):
    rows = ext.shape[1] // 2
    x = jnp.concatenate([ext[links_ref[k, b]] for k in range(links_ref.shape[0])], axis=1)
    main = lax.dot_general(x, high_ref[b], NT, preferred_element_type=F32)
    rest = lax.dot_general(x[:rows], low_ref[b], NT, preferred_element_type=F32)
    return main[:rows] + (main[rows:] + rest)


def first(
    links_ref, tiles_ref, omega_ref, mass_ref, field_ref, high_ref, low_ref, got1, got2, got3, got4,
    dir_ref, base_ref, send1, send2, send3, send4, ext,
):
    blocks, rows, lanes = field_ref.shape
    extend(field_ref, (got1, got2, got3, got4), ext)
    omega, real = frequency_rows(omega_ref, rows, lanes)
    sign = jnp.where(real, -omega, omega)
    for b in range(blocks):
        u = field_ref[b]
        au = curl_row(b, links_ref, high_ref, low_ref, ext)
        au = au + sign * mass_ref[b : b + 1] * other(u)
        resid = u - au
        direction = C1 * u + C2 * resid
        dir_ref[b] = direction
        base_ref[b] = u + direction + C3 * direction + C4 * resid
    pick(tiles_ref, dir_ref, (send1, send2, send3, send4))


def second(
    scale, links_ref, omega_ref, mass_ref, dir_ref, base_ref, high_ref, low_ref, got1, got2, got3, got4,
    cells_ref, fwd_ref, adj_ref, grad_ref, ext, table,
):
    blocks, rows, lanes = dir_ref.shape
    half = rows // 2
    extend(dir_ref, (got1, got2, got3, got4), ext)
    omega, real = frequency_rows(omega_ref, rows, lanes)
    sign = jnp.where(real, -omega, omega)
    for b in range(blocks):
        au = curl_row(b, links_ref, high_ref, low_ref, ext)
        au = au + sign * mass_ref[b : b + 1] * other(dir_ref[b])
        x = base_ref[b] - C4 * au
        efield, lfield = x[:half], x[half:]
        fwd_ref[pl.ds(b, half, stride=blocks), :] = efield
        adj_ref[pl.ds(b, half, stride=blocks), :] = lfield
        prod = omega[:half] * efield * other(lfield)
        table[b : b + 1] = jnp.sum(prod, axis=0, keepdims=True)
    edges, cells = cells_ref.shape
    padded = -(-edges // 8) * 8
    for c in range(cells // lanes):
        index = cells_ref[:, c * lanes : (c + 1) * lanes]
        fill = jnp.full((padded - edges, lanes), -1, jnp.int32)
        index = jnp.concatenate([index, fill], axis=0)
        total = None
        for e in range(0, padded, 8):
            block, lane = index[e : e + 8] >> 7, index[e : e + 8] & 127
            found = jnp.zeros((8, lanes), F32)
            for b in range(blocks):
                row = jnp.broadcast_to(table[b : b + 1], (8, lanes))
                value = jnp.take_along_axis(row, lane, axis=1, mode="promise_in_bounds")
                found = jnp.where(block == b, value, found)
            total = found if total is None else total + found
        grad_ref[c : c + 1] = jnp.sum(total, axis=0, keepdims=True) * scale


def local(
    fwd_source, adj_source, curl_blocks, block_links, tile_lists, edge_mass, omega, cell_edges, log_cond
):
    count, comps, blocks, lanes = fwd_source.shape
    rounds, tiles = tile_lists.shape
    links = block_links.shape[1]
    half = count * comps
    rows = 2 * half
    field_shape = pltpu.VMEM((blocks, rows, lanes), F32)
    tile_shape = pltpu.VMEM((tiles, rows, lanes), F32)
    matrix_shape = pltpu.VMEM((blocks, lanes, links * lanes), BF16)
    flat = (half * blocks, lanes)
    ext = pltpu.VMEM((blocks + rounds * tiles, 2 * rows, lanes), BF16)
    links_t = block_links.T

    field, *sends = pl.pallas_call(
        prepare,
        out_shape=[field_shape] + [tile_shape] * rounds,
        in_specs=[SM, VM, VM],
        out_specs=[VM] * (1 + rounds),
        compiler_params=params(8),
        name="prepare",
    )(tile_lists, fwd_source.reshape(flat), adj_source.reshape(flat))

    def trade(sends):
        got = [None] * rounds
        for r in (2, 1, 3, 0):
            got[r] = swapped(sends[r], "dom", 2**r)
        return [near(g) for g in got]

    got = trade(sends)
    high, low = pl.pallas_call(
        split,
        out_shape=[matrix_shape] * 2,
        in_specs=[pl.BlockSpec(memory_space=pl.ANY)],
        out_specs=[VM] * 2,
        scratch_shapes=[pltpu.VMEM(curl_blocks.shape, F32), pltpu.SemaphoreType.DMA((blocks,))],
        compiler_params=params(32),
        cost_estimate=cost(8 << 20, 16 << 20),
        name="split",
    )(curl_blocks)
    high, low = near(high), near(low)
    field = near(field)
    direction, base, *sends = pl.pallas_call(
        first,
        out_shape=[field_shape] * 2 + [tile_shape] * rounds,
        in_specs=[SM] * 3 + [VM] * (4 + rounds),
        out_specs=[VM] * (2 + rounds),
        scratch_shapes=[ext],
        compiler_params=params(32),
        name="first",
    )(links_t, tile_lists, omega, edge_mass, field, high, low, *got)
    got = trade(sends)
    scale = 1.0 / math.sqrt(24.0 * count * lax.axis_size("freq"))
    efield, lfield, grad = pl.pallas_call(
        lambda *refs: second(scale, *refs),
        out_shape=[
            jax.ShapeDtypeStruct(flat, F32),
            jax.ShapeDtypeStruct(flat, F32),
            jax.ShapeDtypeStruct((log_cond.shape[0] // lanes, lanes), F32),
        ],
        in_specs=[SM] * 2 + [VM] * (6 + rounds),
        out_specs=[VM] * 3,
        scratch_shapes=[ext, pltpu.VMEM((blocks, lanes), F32)],
        compiler_params=params(32),
        name="second",
    )(links_t, omega, edge_mass, near(direction), near(base), high, low, *got, cell_edges)
    for mask in (2, 6, 1):
        grad = grad + swapped(grad, "freq", mask)
    grad = grad.reshape(log_cond.shape)
    model_next = log_cond - 0.5 * grad / jnp.sqrt(grad * grad + 1.0)
    shape = fwd_source.shape
    return efield.reshape(shape), lfield.reshape(shape), model_next


def solution(mesh):
    field = P("freq", None, "dom", None)
    in_specs = (
        field,
        field,
        P("dom", None, None, None),
        P("dom", None),
        P("dom", None),
        P("dom", None),
        P("freq"),
        P(None, "dom"),
        P("dom"),
    )
    out_specs = (field, field, P("dom"))
    return jax.shard_map(local, mesh=mesh, in_specs=in_specs, out_specs=out_specs, check_vma=False)
```

time: 183 us -> 50.5 us (0.28)
  local copies, waits for them, and re-layouts: 84.3 us -> 5.89 us
  matrix products: 37 us -> 0 us
  blocking collectives: 31.5 us -> 0 us
  Pallas kernels: 0 us -> 10.5 us
  waiting for transfers between devices: 6.85 us -> 11.8 us
  other arithmetic: 5.52 us -> 0.61 us
  starting transfers between devices: 16 us -> 20.4 us
    gather x22 -> x0, local copies, waits for them, and re-layouts: 80.1 us -> none  [the longest x2 68 us: local(): jnp.take(edge_term, cell_edges.reshape(-1), axis=0)]
    dot_general x4 -> x0, matrix products: 37 us -> none  [operate(): jnp.einsum('blij,blmj->bmi', curl_blocks, gathered, precision=lax.Precisi...]
    psum x1 -> x0, blocking collectives: 31.5 us -> none  [local(): grad = lax.psum(partial_grad, 'freq')]
    pallas_call x0 -> x4, Pallas kernels: none -> 10.5 us  [the longest x1 4.1 us: local(): pl.pallas_call(lambda *refs: second(scale, *refs), out_shape=[jax.ShapeDt...]
    ppermute x16 -> x11, waiting for transfers between devices: 6.85 us -> 11.8 us  [swapped(): return lax.ppermute(value, axis, pairs)]
    ppermute x16 -> x11, starting transfers between devices: 16 us -> 20.4 us  [swapped(): return lax.ppermute(value, axis, pairs)]
    unnamed x26 -> x20, local copies, waits for them, and re-layouts: 1.78 us -> 5.89 us
    transpose x2 -> x0, local copies, waits for them, and re-layouts: 1.99 us -> none  [to_rows(): moved = jnp.transpose(fields, (3, 0, 1, 2, 4))]
  transfers between devices with their start and end apart: 16 -> 11, of which waited for: 4 -> 5; matrix products, arithmetic and copies ran while one was open for 4% -> 0% of each run, Pallas kernels for 0% -> 5%
where the time goes in v1:
time: 50.5 us; the launch traced here: 50.1 us
  starting transfers between devices  20.4 us (40%)
  waiting for transfers between devices  11.8 us (23%)
  Pallas kernels  10.5 us (21%)
  local copies, waits for them, and re-layouts  5.89 us (12%)
  between operations  0.77 us (2%)
  other arithmetic  0.61 us (1%)
    ppermute x11, starting transfers between devices, swapped(): return lax.ppermute(value, axis, pairs)  20.4 us
    ppermute x11, waiting for transfers between devices, swapped(): return lax.ppermute(value, axis, pairs)  11.8 us
    unnamed x20, local copies, waits for them, and re-layouts  5.89 us
    pallas_call x1, Pallas kernels, local(): pl.pallas_call(lambda *refs: second(scale, *refs), out_shape=[jax.ShapeDt...  4.1 us
    pallas_call x1, Pallas kernels, local(): pl.pallas_call(first, out_shape=[field_shape] * 2 + [tile_shape] * rounds...  3.34 us
    pallas_call x1, Pallas kernels, local(): pl.pallas_call(split, out_shape=[matrix_shape] * 2, in_specs=[pl.BlockSpe...  2.34 us
  transfers between devices with their start and end apart: 11, of which 5 were waited for; matrix products, arithmetic and copies ran while one was open for 0% of the time, Pallas kernels for 5%

profile of v1, /device:TPU:4, one launch (start us, length us, event | category | flops | bytes accessed | tf_op | source)
XLA Modules:
  0.0 50.1 jit_solution(15367342102556414995)
XLA Ops:
  0.6 0.9 %copy-done.1 = f32[2,4,32,128]{3,2,1,0:T(8,128)S(1)} copy-done((f32[2,4,32,128]{3,2,1,0:T(8,128)S(1)}, f32[2,4,32,128]{3,2,1,0:T(8,128)}, u32[]{:S(2)}) %copy-start.1) | copy-done | bytes 131096
  1.5 0.9 %copy-done.2 = f32[2,4,32,128]{3,2,1,0:T(8,128)S(1)} copy-done((f32[2,4,32,128]{3,2,1,0:T(8,128)S(1)}, f32[2,4,32,128]{3,2,1,0:T(8,128)}, u32[]{:S(2)}) %copy-start.2) | copy-done | bytes 131096
  2.4 0.7 %copy-done.5 = s32[4,16]{1,0:T(4,128)S(1)} copy-done((s32[4,16]{1,0:T(4,128)S(1)}, s32[4,16]{1,0:T(4,128)}, u32[]{:S(2)}) %copy-start.5) | copy-done | bytes 280
  3.1 0.8 %prepare.1 = (f32[32,16,128]{2,1,0:T(8,128)S(1)}, f32[16,16,128]{2,1,0:T(8,128)S(1)}, f32[16,16,128]{2,1,0:T(8,128)S(1)}, f32[16,16,128]{2,1,0:T(8,128)S(1)}, f32[16,16,128]{2,1,0:T(8,128)S(1)}) custom-call(s32[4,16]{1,0:T(4,128)S(1)} %copy-done.5, f32[256,128]{1,0:T(8,128)S(1)} %bitcast.7, f32[256,128]{1,0:T(8,128)S(1)} %bitcast.8), custom_call_target="tpu_custom_call" | custom-call | tf_op jit(solution)/shard_map/prepare/pallas_call | solution.py:182
  3.9 0.1 collective-permute-start
  4.0 2.0 %collective-permute-start.1 = (f32[16,16,128]{2,1,0:T(8,128)S(1)}, f32[16,16,128]{2,1,0:T(8,128)S(1)}, u32[]{:S(2)}, u32[]{:S(2)}) collective-permute-start(f32[16,16,128]{2,1,0:T(8,128)S(1)} %get-tuple-element.23), channel_id=1, source_target_pairs={{0,2},{1,3},{2,0},{3,1},{4,6},{5,7},{6,4},{7,5},{8,10},{9,11},{10,... | collective-permute-start | bytes 393224 | tf_op jit(solution)/shard_map/ppermute | solution.py:27
  6.0 3.3 %collective-permute-start.2 = (f32[16,16,128]{2,1,0:T(8,128)S(1)}, f32[16,16,128]{2,1,0:T(8,128)S(1)}, u32[]{:S(2)}, u32[]{:S(2)}) collective-permute-start(f32[16,16,128]{2,1,0:T(8,128)S(1)} %get-tuple-element.24), channel_id=1, source_target_pairs={{0,4},{1,5},{2,6},{3,7},{4,0},{5,1},{6,2},{7,3},{8,12},{9,13},{10,... | collective-permute-start | bytes 393224 | tf_op jit(solution)/shard_map/ppermute | solution.py:27
  9.3 1.2 %collective-permute-start.3 = (f32[16,16,128]{2,1,0:T(8,128)S(1)}, f32[16,16,128]{2,1,0:T(8,128)S(1)}, u32[]{:S(2)}, u32[]{:S(2)}) collective-permute-start(f32[16,16,128]{2,1,0:T(8,128)S(1)} %get-tuple-element.25), channel_id=1, source_target_pairs={{0,8},{1,9},{2,10},{3,11},{4,12},{5,13},{6,14},{7,15},{8,0},{9,1},... | collective-permute-start | bytes 393224 | tf_op jit(solution)/shard_map/ppermute | solution.py:27
  10.5 3.4 %copy-done = f32[32,4,128,128]{3,2,1,0:T(8,128)S(1)} copy-done((f32[32,4,128,128]{3,2,1,0:T(8,128)S(1)}, f32[32,4,128,128]{3,2,1,0:T(8,128)}, u32[]{:S(2)}) %copy-start) | copy-done | bytes 8388632
  13.9 2.3 %split.1 = (bf16[32,128,512]{2,1,0:T(8,128)(2,1)S(1)}, bf16[32,128,512]{2,1,0:T(8,128)(2,1)S(1)}) custom-call(f32[32,4,128,128]{3,2,1,0:T(8,128)S(1)} %copy-done), custom_call_target="tpu_custom_call" | custom-call | flops 8388608 | bytes 16777216 | tf_op jit(solution)/shard_map/split/pallas_call | solution.py:198
  16.3 3.3 %first.1 = (f32[32,16,128]{2,1,0:T(8,128)S(1)}, f32[32,16,128]{2,1,0:T(8,128)S(1)}, f32[16,16,128]{2,1,0:T(8,128)S(1)}, f32[16,16,128]{2,1,0:T(8,128)S(1)}, f32[...) custom-call(s32[4,32]{1,0:T(4,128)S(1)} %bitcast.9, s32[4,16]{1,0:T(4,128)S(1)} %copy-done.6, f32[2]{0:T(128)S(1)} %copy-done.8, ...), custom_call_target="tpu_custom_call" | custom-call | tf_op jit(solution)/shard_map/first/pallas_call | solution.py:210
  19.8 0.2 collective-permute-start.5
  20.0 2.5 %collective-permute-start.6 = (f32[16,16,128]{2,1,0:T(8,128)S(1)}, f32[16,16,128]{2,1,0:T(8,128)S(1)}, u32[]{:S(2)}, u32[]{:S(2)}) collective-permute-start(f32[16,16,128]{2,1,0:T(8,128)S(1)} %get-tuple-element.30), channel_id=1, source_target_pairs={{0,4},{1,5},{2,6},{3,7},{4,0},{5,1},{6,2},{7,3},{8,12},{9,13},{10,... | collective-permute-start | bytes 393224 | tf_op jit(solution)/shard_map/ppermute | solution.py:27
  22.4 1.2 %collective-permute-start.7 = (f32[16,16,128]{2,1,0:T(8,128)S(1)}, f32[16,16,128]{2,1,0:T(8,128)S(1)}, u32[]{:S(2)}, u32[]{:S(2)}) collective-permute-start(f32[16,16,128]{2,1,0:T(8,128)S(1)} %get-tuple-element.31), channel_id=1, source_target_pairs={{0,8},{1,9},{2,10},{3,11},{4,12},{5,13},{6,14},{7,15},{8,0},{9,1},... | collective-permute-start | bytes 393224 | tf_op jit(solution)/shard_map/ppermute | solution.py:27
  23.6 4.3 %collective-permute-done.5.refs_8_ = f32[16,16,128]{2,1,0:T(8,128)S(1)} collective-permute-done((f32[16,16,128]{2,1,0:T(8,128)S(1)}, f32[16,16,128]{2,1,0:T(8,128)S(1)}, u32[]{:S(2)}, u32[]{:S(2)}) %collective-permute-start.5) | collective-permute-done | bytes 131104 | tf_op jit(solution)/shard_map/ppermute | solution.py:27
  27.9 1.5 %collective-permute-done.6.refs_9_ = f32[16,16,128]{2,1,0:T(8,128)S(1)} collective-permute-done((f32[16,16,128]{2,1,0:T(8,128)S(1)}, f32[16,16,128]{2,1,0:T(8,128)S(1)}, u32[]{:S(2)}, u32[]{:S(2)}) %collective-permute-start.6) | collective-permute-done | bytes 131104 | tf_op jit(solution)/shard_map/ppermute | solution.py:27
  29.4 4.1 %second.1 = (f32[256,128]{1,0:T(8,128)}, f32[256,128]{1,0:T(8,128)}, f32[8,128]{1,0:T(8,128)S(1)}) custom-call(s32[4,32]{1,0:T(4,128)S(1)} %bitcast.10, f32[2]{0:T(128)S(1)} %copy-done.8, f32[32,128]{1,0:T(8,128)S(1)} %copy-done.4, f32[32,16,128]{2,1,0:T(8,128)S(1)} %get-tuple-element.26.refs_3_, f32[32,16,128]{2,1,0:T(8,128)S(1)} %get-tuple-element.27.refs_4_, ...), custom_call_target="tpu_custom_call" | custom-call | tf_op jit(solution)/shard_map/second/pallas_call | solution.py:221
  33.5 1.6 %collective-permute-start.8 = (f32[8,128]{1,0:T(8,128)S(1)}, f32[8,128]{1,0:T(8,128)S(1)}, u32[]{:S(2)}, u32[]{:S(2)}) collective-permute-start(f32[8,128]{1,0:T(8,128)S(1)} %get-tuple-element.34), channel_id=1, source_target_pairs={{0,64},{32,96},{64,0},{96,32},{128,192},{160,224},{192,128},{224,1... | collective-permute-start | bytes 12296 | tf_op jit(solution)/shard_map/ppermute | solution.py:27
  35.1 2.0 %collective-permute-done.8 = f32[8,128]{1,0:T(8,128)S(1)} collective-permute-done((f32[8,128]{1,0:T(8,128)S(1)}, f32[8,128]{1,0:T(8,128)S(1)}, u32[]{:S(2)}, u32[]{:S(2)}) %collective-permute-start.8) | collective-permute-done | bytes 4128 | tf_op jit(solution)/shard_map/ppermute | solution.py:27
  37.1 3.0 %collective-permute-start.9 = (f32[8,128]{1,0:T(8,128)S(1)}, f32[8,128]{1,0:T(8,128)S(1)}, u32[]{:S(2)}, u32[]{:S(2)}) collective-permute-start(f32[8,128]{1,0:T(8,128)S(1)} %add.16), channel_id=1, source_target_pairs={{0,192},{32,224},{64,128},{96,160},{128,64},{160,96},{192,0},{224,... | collective-permute-start | bytes 12296 | tf_op jit(solution)/shard_map/ppermute | solution.py:27
  40.1 1.8 %collective-permute-done.9 = f32[8,128]{1,0:T(8,128)S(1)} collective-permute-done((f32[8,128]{1,0:T(8,128)S(1)}, f32[8,128]{1,0:T(8,128)S(1)}, u32[]{:S(2)}, u32[]{:S(2)}) %collective-permute-start.9) | collective-permute-done | bytes 4128 | tf_op jit(solution)/shard_map/ppermute | solution.py:27
  42.0 5.3 %collective-permute-start.10 = (f32[8,128]{1,0:T(8,128)S(1)}, f32[8,128]{1,0:T(8,128)S(1)}, u32[]{:S(2)}, u32[]{:S(2)}) collective-permute-start(f32[8,128]{1,0:T(8,128)S(1)} %add.17), channel_id=1, source_target_pairs={{0,32},{32,0},{64,96},{96,64},{128,160},{160,128},{192,224},{224,1... | collective-permute-start | bytes 12296 | tf_op jit(solution)/shard_map/ppermute | solution.py:27
  47.3 2.2 %collective-permute-done.10 = f32[8,128]{1,0:T(8,128)S(1)} collective-permute-done((f32[8,128]{1,0:T(8,128)S(1)}, f32[8,128]{1,0:T(8,128)S(1)}, u32[]{:S(2)}, u32[]{:S(2)}) %collective-permute-start.10) | collective-permute-done | bytes 4128 | tf_op jit(solution)/shard_map/ppermute | solution.py:27
  49.5 0.6 %bitcast_subtract_fusion = f32[1024]{0:T(1024)} fusion(f32[1024]{0:T(1024)S(1)} %copy-done.9, f32[8,128]{1,0:T(8,128)S(1)} %add.17, f32[8,128]{1,0:T(8,128)S(1)} %collective-permute-done.10), kind=kLoop, calls=%fused_computation | loop fusion | flops 6144 | bytes 16384 | tf_op jit(solution)/shard_map/sub | solution.py:237
  (25 shorter events, 0.1 us)
Async XLA Ops:
  0.6 0.9 %copy-start.1 = (f32[2,4,32,128]{3,2,1,0:T(8,128)S(1)}, f32[2,4,32,128]{3,2,1,0:T(8,128)}, u32[]{:S(2)}) copy-start(f32[2,4,32,128]{3,2,1,0:T(8,128)} %param.9) | copy-start | bytes 393220
  1.5 0.9 %copy-start.2 = (f32[2,4,32,128]{3,2,1,0:T(8,128)S(1)}, f32[2,4,32,128]{3,2,1,0:T(8,128)}, u32[]{:S(2)}) copy-start(f32[2,4,32,128]{3,2,1,0:T(8,128)} %param.10) | copy-start | bytes 393220
  2.4 0.7 %copy-start.5 = (s32[4,16]{1,0:T(4,128)S(1)}, s32[4,16]{1,0:T(4,128)}, u32[]{:S(2)}) copy-start(s32[4,16]{1,0:T(4,128)} %tiles_ref.3) | copy-start | bytes 772
  3.9 12.3 %collective-permute-start = (f32[16,16,128]{2,1,0:T(8,128)S(1)}, f32[16,16,128]{2,1,0:T(8,128)S(1)}, u32[]{:S(2)}, u32[]{:S(2)}) collective-permute-start(f32[16,16,128]{2,1,0:T(8,128)S(1)} %get-tuple-element.22), channel_id=1, source_target_pairs={{0,1},{1,0},{2,3},{3,2},{4,5},{5,4},{6,7},{7,6},{8,9},{9,8},{10,11... | collective-permute-start | bytes 393224 | tf_op jit(solution)/shard_map/ppermute | solution.py:27
  4.0 12.2 %collective-permute-start.1 = (f32[16,16,128]{2,1,0:T(8,128)S(1)}, f32[16,16,128]{2,1,0:T(8,128)S(1)}, u32[]{:S(2)}, u32[]{:S(2)}) collective-permute-start(f32[16,16,128]{2,1,0:T(8,128)S(1)} %get-tuple-element.23), channel_id=1, source_target_pairs={{0,2},{1,3},{2,0},{3,1},{4,6},{5,7},{6,4},{7,5},{8,10},{9,11},{10,... | collective-permute-start | bytes 393224 | tf_op jit(solution)/shard_map/ppermute | solution.py:27
  6.0 10.2 %collective-permute-start.2 = (f32[16,16,128]{2,1,0:T(8,128)S(1)}, f32[16,16,128]{2,1,0:T(8,128)S(1)}, u32[]{:S(2)}, u32[]{:S(2)}) collective-permute-start(f32[16,16,128]{2,1,0:T(8,128)S(1)} %get-tuple-element.24), channel_id=1, source_target_pairs={{0,4},{1,5},{2,6},{3,7},{4,0},{5,1},{6,2},{7,3},{8,12},{9,13},{10,... | collective-permute-start | bytes 393224 | tf_op jit(solution)/shard_map/ppermute | solution.py:27
  9.3 7.0 %collective-permute-start.3 = (f32[16,16,128]{2,1,0:T(8,128)S(1)}, f32[16,16,128]{2,1,0:T(8,128)S(1)}, u32[]{:S(2)}, u32[]{:S(2)}) collective-permute-start(f32[16,16,128]{2,1,0:T(8,128)S(1)} %get-tuple-element.25), channel_id=1, source_target_pairs={{0,8},{1,9},{2,10},{3,11},{4,12},{5,13},{6,14},{7,15},{8,0},{9,1},... | collective-permute-start | bytes 393224 | tf_op jit(solution)/shard_map/ppermute | solution.py:27
  10.5 3.4 %copy-start = (f32[32,4,128,128]{3,2,1,0:T(8,128)S(1)}, f32[32,4,128,128]{3,2,1,0:T(8,128)}, u32[]{:S(2)}) copy-start(f32[32,4,128,128]{3,2,1,0:T(8,128)} %curl_ref.1) | copy-start | bytes 25165828
  13.8 2.4 %copy-start.4 = (f32[32,128]{1,0:T(8,128)S(1)}, f32[32,128]{1,0:T(8,128)}, u32[]{:S(2)}) copy-start(f32[32,128]{1,0:T(8,128)} %refs_2_.1) | copy-start | bytes 49156
  13.9 2.4 %copy-start.6 = (s32[4,16]{1,0:T(4,128)S(1)}, s32[4,16]{1,0:T(4,128)}, u32[]{:S(2)}) copy-start(s32[4,16]{1,0:T(4,128)} %tiles_ref.3) | copy-start | bytes 772
  13.9 2.4 %copy-start.7 = (s32[32,4]{0,1:T(4,128)S(1)}, s32[32,4]{0,1:T(4,128)}, u32[]{:S(2)}) copy-start(s32[32,4]{0,1:T(4,128)} %param.12) | copy-start | bytes 1540
  13.9 2.4 %copy-start.8 = (f32[2]{0:T(128)S(1)}, f32[2]{0:T(128)}, u32[]{:S(2)}) copy-start(f32[2]{0:T(128)} %refs_1_.1) | copy-start | bytes 28
  16.3 13.1 %copy-start.3 = (s32[12,1024]{1,0:T(8,128)S(1)}, s32[12,1024]{1,0:T(8,128)}, u32[]{:S(2)}) copy-start(s32[12,1024]{1,0:T(8,128)} %refs_11_.1) | copy-start | bytes 147460
  19.7 4.0 %collective-permute-start.4 = (f32[16,16,128]{2,1,0:T(8,128)S(1)}, f32[16,16,128]{2,1,0:T(8,128)S(1)}, u32[]{:S(2)}, u32[]{:S(2)}) collective-permute-start(f32[16,16,128]{2,1,0:T(8,128)S(1)} %get-tuple-element.28), channel_id=1, source_target_pairs={{0,1},{1,0},{2,3},{3,2},{4,5},{5,4},{6,7},{7,6},{8,9},{9,8},{10,11... | collective-permute-start | bytes 393224 | tf_op jit(solution)/shard_map/ppermute | solution.py:27
  19.8 8.2 %collective-permute-start.5 = (f32[16,16,128]{2,1,0:T(8,128)S(1)}, f32[16,16,128]{2,1,0:T(8,128)S(1)}, u32[]{:S(2)}, u32[]{:S(2)}) collective-permute-start(f32[16,16,128]{2,1,0:T(8,128)S(1)} %get-tuple-element.29), channel_id=1, source_target_pairs={{0,2},{1,3},{2,0},{3,1},{4,6},{5,7},{6,4},{7,5},{8,10},{9,11},{10,... | collective-permute-start | bytes 393224 | tf_op jit(solution)/shard_map/ppermute | solution.py:27
  20.0 9.5 %collective-permute-start.6 = (f32[16,16,128]{2,1,0:T(8,128)S(1)}, f32[16,16,128]{2,1,0:T(8,128)S(1)}, u32[]{:S(2)}, u32[]{:S(2)}) collective-permute-start(f32[16,16,128]{2,1,0:T(8,128)S(1)} %get-tuple-element.30), channel_id=1, source_target_pairs={{0,4},{1,5},{2,6},{3,7},{4,0},{5,1},{6,2},{7,3},{8,12},{9,13},{10,... | collective-permute-start | bytes 393224 | tf_op jit(solution)/shard_map/ppermute | solution.py:27
  22.4 7.0 %collective-permute-start.7 = (f32[16,16,128]{2,1,0:T(8,128)S(1)}, f32[16,16,128]{2,1,0:T(8,128)S(1)}, u32[]{:S(2)}, u32[]{:S(2)}) collective-permute-start(f32[16,16,128]{2,1,0:T(8,128)S(1)} %get-tuple-element.31), channel_id=1, source_target_pairs={{0,8},{1,9},{2,10},{3,11},{4,12},{5,13},{6,14},{7,15},{8,0},{9,1},... | collective-permute-start | bytes 393224 | tf_op jit(solution)/shard_map/ppermute | solution.py:27
  29.4 20.1 %copy-start.9 = (f32[1024]{0:T(1024)S(1)}, f32[1024]{0:T(1024)}, u32[]{:S(2)}) copy-start(f32[1024]{0:T(1024)} %param.17) | copy-start | bytes 12292
  33.5 3.6 %collective-permute-start.8 = (f32[8,128]{1,0:T(8,128)S(1)}, f32[8,128]{1,0:T(8,128)S(1)}, u32[]{:S(2)}, u32[]{:S(2)}) collective-permute-start(f32[8,128]{1,0:T(8,128)S(1)} %get-tuple-element.34), channel_id=1, source_target_pairs={{0,64},{32,96},{64,0},{96,32},{128,192},{160,224},{192,128},{224,1... | collective-permute-start | bytes 12296 | tf_op jit(solution)/shard_map/ppermute | solution.py:27
  37.1 4.8 %collective-permute-start.9 = (f32[8,128]{1,0:T(8,128)S(1)}, f32[8,128]{1,0:T(8,128)S(1)}, u32[]{:S(2)}, u32[]{:S(2)}) collective-permute-start(f32[8,128]{1,0:T(8,128)S(1)} %add.16), channel_id=1, source_target_pairs={{0,192},{32,224},{64,128},{96,160},{128,64},{160,96},{192,0},{224,... | collective-permute-start | bytes 12296 | tf_op jit(solution)/shard_map/ppermute | solution.py:27
  42.0 7.5 %collective-permute-start.10 = (f32[8,128]{1,0:T(8,128)S(1)}, f32[8,128]{1,0:T(8,128)S(1)}, u32[]{:S(2)}, u32[]{:S(2)}) collective-permute-start(f32[8,128]{1,0:T(8,128)S(1)} %add.17), channel_id=1, source_target_pairs={{0,32},{32,0},{64,96},{96,64},{128,160},{160,128},{192,224},{224,1... | collective-permute-start | bytes 12296 | tf_op jit(solution)/shard_map/ppermute | solution.py:27

commit v2 on v1

--- a/solution.py
+++ b/solution.py
@@ -19,6 +19,8 @@
 F32, BF16 = jnp.float32, jnp.bfloat16
 VM = pl.BlockSpec(memory_space=pltpu.VMEM)
 SM = pl.BlockSpec(memory_space=pltpu.SMEM)
+HB = pl.BlockSpec(memory_space=pltpu.HBM)
+DMA = pltpu.SemaphoreType.DMA
 NT = (((1,), (1,)), ((), ()))
 
 
@@ -29,6 +31,10 @@
 
 def near(value):
     return pltpu.with_memory_space_constraint(value, pltpu.VMEM)
+
+
+def far(value):
+    return pltpu.with_memory_space_constraint(value, pltpu.HBM)
 
 
 def params(mib):
@@ -66,28 +72,40 @@
             send_ref[t] = field_ref[tiles_ref[r, t]]
 
 
-def prepare(tiles_ref, fwd_ref, adj_ref, field_ref, *send_refs):
+def prepare(
+    tiles_hbm, fwd_hbm, adj_hbm, field_ref, send1, send2, send3, send4, tiles_ref, fwd_ref, adj_ref, sems
+):
     blocks, rows, _ = field_ref.shape
     half = rows // 2
+    pairs = ((tiles_hbm, tiles_ref), (fwd_hbm, fwd_ref), (adj_hbm, adj_ref))
+    copies = [pltpu.make_async_copy(a, b, sems.at[i]) for i, (a, b) in enumerate(pairs)]
+    for copy in copies:
+        copy.start()
+    for copy in copies:
+        copy.wait()
     for b in range(blocks):
         field_ref[b, :half] = fwd_ref[pl.ds(b, half, stride=blocks), :]
         field_ref[b, half:] = adj_ref[pl.ds(b, half, stride=blocks), :]
-    pick(tiles_ref, field_ref, send_refs)
-
-
-def split(curl_ref, high_ref, low_ref, buf, sems):
+    pick(tiles_ref, field_ref, (send1, send2, send3, send4))
+
+
+def split(curl_ref, matrix_ref, buf, sems):
     blocks, links, width, _ = curl_ref.shape
+    groups = sems.shape[0]
+    per = blocks // groups
+    chunks = [pl.ds(g * per, per) for g in range(groups)]
     copies = [
-        pltpu.make_async_copy(curl_ref.at[b], buf.at[b], sems.at[b]) for b in range(blocks)
+        pltpu.make_async_copy(curl_ref.at[c], buf.at[c], sems.at[g]) for g, c in enumerate(chunks)
     ]
     for copy in copies:
         copy.start()
     for b in range(blocks):
-        copies[b].wait()
+        if b % per == 0:
+            copies[b // per].wait()
         for k in range(links):
             high, low = halves(buf[b, k])
-            high_ref[b, :, k * width : (k + 1) * width] = high
-            low_ref[b, :, k * width : (k + 1) * width] = low
+            matrix_ref[b, k * width : (k + 1) * width, :width] = high.T
+            matrix_ref[b, k * width : (k + 1) * width, width:] = low.T
 
 
 def extend(field_ref, got_refs, ext):
@@ -101,16 +119,15 @@
             at += 1
 
 
-def curl_row(b, links_ref, high_ref, low_ref, ext):
-    rows = ext.shape[1] // 2
+def curl_row(b, links_ref, matrix_ref, ext):
+    rows, width = ext.shape[1] // 2, ext.shape[2]
     x = jnp.concatenate([ext[links_ref[k, b]] for k in range(links_ref.shape[0])], axis=1)
-    main = lax.dot_general(x, high_ref[b], NT, preferred_element_type=F32)
-    rest = lax.dot_general(x[:rows], low_ref[b], NT, preferred_element_type=F32)
-    return main[:rows] + (main[rows:] + rest)
+    y = jnp.dot(x, matrix_ref[b], preferred_element_type=F32)
+    return y[:rows, :width] + (y[rows:, :width] + y[:rows, width:] + y[rows:, width:])
 
 
 def first(
-    links_ref, tiles_ref, omega_ref, mass_ref, field_ref, high_ref, low_ref, got1, got2, got3, got4,
+    links_ref, tiles_ref, omega_ref, mass_ref, field_ref, matrix_ref, got1, got2, got3, got4,
     dir_ref, base_ref, send1, send2, send3, send4, ext,
 ):
     blocks, rows, lanes = field_ref.shape
@@ -119,7 +136,7 @@
     sign = jnp.where(real, -omega, omega)
     for b in range(blocks):
         u = field_ref[b]
-        au = curl_row(b, links_ref, high_ref, low_ref, ext)
+        au = curl_row(b, links_ref, matrix_ref, ext)
         au = au + sign * mass_ref[b : b + 1] * other(u)
         resid = u - au
         direction = C1 * u + C2 * resid
@@ -129,8 +146,8 @@
 
 
 def second(
-    scale, links_ref, omega_ref, mass_ref, dir_ref, base_ref, high_ref, low_ref, got1, got2, got3, got4,
-    cells_ref, fwd_ref, adj_ref, grad_ref, ext, table,
+    scale, links_ref, omega_ref, mass_ref, dir_ref, base_ref, matrix_ref, got1, got2, got3, got4,
+    cells_ref, fwd_hbm, adj_hbm, grad_ref, ext, table, fwd_ref, adj_ref, sems,
 ):
     blocks, rows, lanes = dir_ref.shape
     half = rows // 2
@@ -138,7 +155,7 @@
     omega, real = frequency_rows(omega_ref, rows, lanes)
     sign = jnp.where(real, -omega, omega)
     for b in range(blocks):
-        au = curl_row(b, links_ref, high_ref, low_ref, ext)
+        au = curl_row(b, links_ref, matrix_ref, ext)
         au = au + sign * mass_ref[b : b + 1] * other(dir_ref[b])
         x = base_ref[b] - C4 * au
         efield, lfield = x[:half], x[half:]
@@ -146,6 +163,12 @@
         adj_ref[pl.ds(b, half, stride=blocks), :] = lfield
         prod = omega[:half] * efield * other(lfield)
         table[b : b + 1] = jnp.sum(prod, axis=0, keepdims=True)
+    copies = [
+        pltpu.make_async_copy(fwd_ref, fwd_hbm, sems.at[0]),
+        pltpu.make_async_copy(adj_ref, adj_hbm, sems.at[1]),
+    ]
+    for copy in copies:
+        copy.start()
     edges, cells = cells_ref.shape
     padded = -(-edges // 8) * 8
     for c in range(cells // lanes):
@@ -162,6 +185,8 @@
                 found = jnp.where(block == b, value, found)
             total = found if total is None else total + found
         grad_ref[c : c + 1] = jnp.sum(total, axis=0, keepdims=True) * scale
+    for copy in copies:
+        copy.wait()
 
 
 def local(
@@ -172,21 +197,23 @@
     links = block_links.shape[1]
     half = count * comps
     rows = 2 * half
+    flat = (half * blocks, lanes)
     field_shape = pltpu.VMEM((blocks, rows, lanes), F32)
     tile_shape = pltpu.VMEM((tiles, rows, lanes), F32)
-    matrix_shape = pltpu.VMEM((blocks, lanes, links * lanes), BF16)
-    flat = (half * blocks, lanes)
+    flat_shape = pltpu.VMEM(flat, F32)
+    matrix_shape = pltpu.VMEM((blocks, links * lanes, 2 * lanes), BF16)
     ext = pltpu.VMEM((blocks + rounds * tiles, 2 * rows, lanes), BF16)
     links_t = block_links.T
 
     field, *sends = pl.pallas_call(
         prepare,
         out_shape=[field_shape] + [tile_shape] * rounds,
-        in_specs=[SM, VM, VM],
+        in_specs=[HB] * 3,
         out_specs=[VM] * (1 + rounds),
+        scratch_shapes=[pltpu.SMEM(tile_lists.shape, jnp.int32), flat_shape, flat_shape, DMA((3,))],
         compiler_params=params(8),
         name="prepare",
-    )(tile_lists, fwd_source.reshape(flat), adj_source.reshape(flat))
+    )(far(tile_lists), far(fwd_source.reshape(flat)), far(adj_source.reshape(flat)))
 
     def trade(sends):
         got = [None] * rounds
@@ -195,44 +222,44 @@
         return [near(g) for g in got]
 
     got = trade(sends)
-    high, low = pl.pallas_call(
+    matrix = pl.pallas_call(
         split,
-        out_shape=[matrix_shape] * 2,
-        in_specs=[pl.BlockSpec(memory_space=pl.ANY)],
-        out_specs=[VM] * 2,
-        scratch_shapes=[pltpu.VMEM(curl_blocks.shape, F32), pltpu.SemaphoreType.DMA((blocks,))],
+        out_shape=matrix_shape,
+        in_specs=[HB],
+        out_specs=VM,
+        scratch_shapes=[pltpu.VMEM(curl_blocks.shape, F32), DMA((blocks // 4,))],
         compiler_params=params(32),
         cost_estimate=cost(8 << 20, 16 << 20),
         name="split",
-    )(curl_blocks)
-    high, low = near(high), near(low)
-    field = near(field)
+    )(far(curl_blocks))
+    matrix = near(matrix)
     direction, base, *sends = pl.pallas_call(
         first,
         out_shape=[field_shape] * 2 + [tile_shape] * rounds,
-        in_specs=[SM] * 3 + [VM] * (4 + rounds),
+        in_specs=[SM] * 3 + [VM] * (3 + rounds),
         out_specs=[VM] * (2 + rounds),
         scratch_shapes=[ext],
         compiler_params=params(32),
         name="first",
-    )(links_t, tile_lists, omega, edge_mass, field, high, low, *got)
+    )(links_t, tile_lists, omega, edge_mass, near(field), matrix, *got)
     got = trade(sends)
     scale = 1.0 / math.sqrt(24.0 * count * lax.axis_size("freq"))
     efield, lfield, grad = pl.pallas_call(
         lambda *refs: second(scale, *refs),
         out_shape=[
-            jax.ShapeDtypeStruct(flat, F32),
-            jax.ShapeDtypeStruct(flat, F32),
-            jax.ShapeDtypeStruct((log_cond.shape[0] // lanes, lanes), F32),
+            pltpu.HBM(flat, F32),
+            pltpu.HBM(flat, F32),
+            pltpu.VMEM((log_cond.shape[0] // lanes, lanes), F32),
         ],
-        in_specs=[SM] * 2 + [VM] * (6 + rounds),
-        out_specs=[VM] * 3,
-        scratch_shapes=[ext, pltpu.VMEM((blocks, lanes), F32)],
+        in_specs=[SM] * 2 + [VM] * (5 + rounds),
+        out_specs=[HB, HB, VM],
+        scratch_shapes=[ext, pltpu.VMEM((blocks, lanes), F32), flat_shape, flat_shape, DMA((2,))],
         compiler_params=params(32),
         name="second",
-    )(links_t, omega, edge_mass, near(direction), near(base), high, low, *got, cell_edges)
-    for mask in (2, 6, 1):
-        grad = grad + swapped(grad, "freq", mask)
+    )(links_t, omega, edge_mass, near(direction), near(base), matrix, *got, cell_edges)
+    got = [swapped(grad, "freq", mask) for mask in (2, 6, 4)]
+    grad = grad + got[0] + got[1] + got[2]
+    grad = grad + swapped(grad, "freq", 1)
     grad = grad.reshape(log_cond.shape)
     model_next = log_cond - 0.5 * grad / jnp.sqrt(grad * grad + 1.0)
     shape = fwd_source.shape

time: 50.5 us -> 45.6 us (0.903)
  local copies, waits for them, and re-layouts: 5.89 us -> 0.03 us
  waiting for transfers between devices: 11.8 us -> 12.5 us
  starting transfers between devices: 20.4 us -> 21 us
    unnamed x20 -> x12, local copies, waits for them, and re-layouts: 5.89 us -> 0.03 us
    pallas_call x1, Pallas kernels: 3.34 us -> 2.3 us  [local(): pl.pallas_call(first, out_shape=[field_shape] * 2 + [tile_shape] * rounds...]
    ppermute x11 -> x12, waiting for transfers between devices: 11.8 us -> 12.5 us  [swapped(): return lax.ppermute(value, axis, pairs)]
    pallas_call x2, Pallas kernels: 6.44 us -> 7.03 us  [the longest x1 3.92 us: local(): pl.pallas_call(split, out_shape=matrix_shape, in_specs=[HB], out_specs=VM...]
    ppermute x11 -> x12, starting transfers between devices: 20.4 us -> 21 us  [swapped(): return lax.ppermute(value, axis, pairs)]
  transfers between devices with their start and end apart: 11 -> 12, of which waited for: 5 -> 6; matrix products, arithmetic and copies ran while one was open for 0% -> 0% of each run, Pallas kernels for 5% -> 9%
where the time goes in v2:
time: 45.6 us; the launch traced here: 45.5 us
  starting transfers between devices  21 us (46%)
  waiting for transfers between devices  12.5 us (27%)
  Pallas kernels  10.5 us (23%)
  between operations  0.75 us (2%)
  other arithmetic  0.61 us (1%)
    ppermute x12, starting transfers between devices, swapped(): return lax.ppermute(value, axis, pairs)  21 us
    ppermute x12, waiting for transfers between devices, swapped(): return lax.ppermute(value, axis, pairs)  12.5 us
    pallas_call x1, Pallas kernels, local(): pl.pallas_call(split, out_shape=matrix_shape, in_specs=[HB], out_specs=VM...  3.92 us
    pallas_call x1, Pallas kernels, local(): pl.pallas_call(lambda *refs: second(scale, *refs), out_shape=[pltpu.HBM(f...  3.1 us
    pallas_call x1, Pallas kernels, local(): pl.pallas_call(first, out_shape=[field_shape] * 2 + [tile_shape] * rounds...  2.3 us
    pallas_call x1, Pallas kernels, local(): pl.pallas_call(prepare, out_shape=[field_shape] + [tile_shape] * rounds,...  1.19 us
  transfers between devices with their start and end apart: 12, of which 6 were waited for; matrix products, arithmetic and copies ran while one was open for 0% of the time, Pallas kernels for 9%

profile of v2, /device:TPU:4, one launch (start us, length us, event | category | flops | bytes accessed | tf_op | source)
XLA Modules:
  0.0 45.5 jit_solution(16710526325114796393)
XLA Ops:
  0.6 1.2 %prepare.1 = (f32[32,16,128]{2,1,0:T(8,128)S(1)}, f32[16,16,128]{2,1,0:T(8,128)S(1)}, f32[16,16,128]{2,1,0:T(8,128)S(1)}, f32[16,16,128]{2,1,0:T(8,128)S(1)}, f32[16,16,128]{2,1,0:T(8,128)S(1)}) custom-call(s32[4,16]{1,0:T(4,128)} %tiles_ref.1, f32[256,128]{1,0:T(8,128)} %bitcast.9, f32[256,128]{1,0:T(8,128)} %bitcast.10), custom_call_target="tpu_custom_call" | custom-call | tf_op jit(solution)/shard_map/prepare/pallas_call | solution.py:208
  1.8 0.1 collective-permute-start
  1.9 2.0 %collective-permute-start.1 = (f32[16,16,128]{2,1,0:T(8,128)S(1)}, f32[16,16,128]{2,1,0:T(8,128)S(1)}, u32[]{:S(2)}, u32[]{:S(2)}) collective-permute-start(f32[16,16,128]{2,1,0:T(8,128)S(1)} %get-tuple-element.19), channel_id=1, source_target_pairs={{0,2},{1,3},{2,0},{3,1},{4,6},{5,7},{6,4},{7,5},{8,10},{9,11},{10,... | collective-permute-start | bytes 393224 | tf_op jit(solution)/shard_map/ppermute | solution.py:29
  3.9 3.3 %collective-permute-start.2 = (f32[16,16,128]{2,1,0:T(8,128)S(1)}, f32[16,16,128]{2,1,0:T(8,128)S(1)}, u32[]{:S(2)}, u32[]{:S(2)}) collective-permute-start(f32[16,16,128]{2,1,0:T(8,128)S(1)} %get-tuple-element.20), channel_id=1, source_target_pairs={{0,4},{1,5},{2,6},{3,7},{4,0},{5,1},{6,2},{7,3},{8,12},{9,13},{10,... | collective-permute-start | bytes 393224 | tf_op jit(solution)/shard_map/ppermute | solution.py:29
  7.2 1.3 %collective-permute-start.3 = (f32[16,16,128]{2,1,0:T(8,128)S(1)}, f32[16,16,128]{2,1,0:T(8,128)S(1)}, u32[]{:S(2)}, u32[]{:S(2)}) collective-permute-start(f32[16,16,128]{2,1,0:T(8,128)S(1)} %get-tuple-element.21), channel_id=1, source_target_pairs={{0,8},{1,9},{2,10},{3,11},{4,12},{5,13},{6,14},{7,15},{8,0},{9,1},... | collective-permute-start | bytes 393224 | tf_op jit(solution)/shard_map/ppermute | solution.py:29
  8.5 3.9 %split.1.matrix_ref.refs_5_ = bf16[32,512,256]{2,1,0:T(8,128)(2,1)S(1)} custom-call(f32[32,4,128,128]{3,2,1,0:T(8,128)} %curl_ref.1), custom_call_target="tpu_custom_call" | custom-call | flops 8388608 | bytes 16777216 | tf_op jit(solution)/shard_map/split/pallas_call | solution.py:225
  12.4 0.0 copy-start
  12.5 1.4 %collective-permute-done.2.got3 = f32[16,16,128]{2,1,0:T(8,128)S(1)} collective-permute-done((f32[16,16,128]{2,1,0:T(8,128)S(1)}, f32[16,16,128]{2,1,0:T(8,128)S(1)}, u32[]{:S(2)}, u32[]{:S(2)}) %collective-permute-start.2) | collective-permute-done | bytes 131104 | tf_op jit(solution)/shard_map/ppermute | solution.py:29
  13.9 0.0 copy-start.5
  13.9 2.3 %first.1 = (f32[32,16,128]{2,1,0:T(8,128)S(1)}, f32[32,16,128]{2,1,0:T(8,128)S(1)}, f32[16,16,128]{2,1,0:T(8,128)S(1)}, f32[16,16,128]{2,1,0:T(8,128)S(1)}, f32[...) custom-call(s32[4,32]{1,0:T(4,128)S(1)} %bitcast.7, s32[4,16]{1,0:T(4,128)S(1)} %copy-done.2, f32[2]{0:T(128)S(1)} %copy-done.4, ...), custom_call_target="tpu_custom_call" | custom-call | tf_op jit(solution)/shard_map/first/pallas_call | solution.py:236
  16.2 0.1 collective-permute-start.4
  16.3 0.4 collective-permute-start.5
  16.7 2.6 %collective-permute-start.6 = (f32[16,16,128]{2,1,0:T(8,128)S(1)}, f32[16,16,128]{2,1,0:T(8,128)S(1)}, u32[]{:S(2)}, u32[]{:S(2)}) collective-permute-start(f32[16,16,128]{2,1,0:T(8,128)S(1)} %get-tuple-element.26), channel_id=1, source_target_pairs={{0,4},{1,5},{2,6},{3,7},{4,0},{5,1},{6,2},{7,3},{8,12},{9,13},{10,... | collective-permute-start | bytes 393224 | tf_op jit(solution)/shard_map/ppermute | solution.py:29
  19.3 1.2 %collective-permute-start.7 = (f32[16,16,128]{2,1,0:T(8,128)S(1)}, f32[16,16,128]{2,1,0:T(8,128)S(1)}, u32[]{:S(2)}, u32[]{:S(2)}) collective-permute-start(f32[16,16,128]{2,1,0:T(8,128)S(1)} %get-tuple-element.27), channel_id=1, source_target_pairs={{0,8},{1,9},{2,10},{3,11},{4,12},{5,13},{6,14},{7,15},{8,0},{9,1},... | collective-permute-start | bytes 393224 | tf_op jit(solution)/shard_map/ppermute | solution.py:29
  20.5 4.2 %collective-permute-done.5.refs_7_ = f32[16,16,128]{2,1,0:T(8,128)S(1)} collective-permute-done((f32[16,16,128]{2,1,0:T(8,128)S(1)}, f32[16,16,128]{2,1,0:T(8,128)S(1)}, u32[]{:S(2)}, u32[]{:S(2)}) %collective-permute-start.5) | collective-permute-done | bytes 131104 | tf_op jit(solution)/shard_map/ppermute | solution.py:29
  24.7 1.3 %collective-permute-done.6.refs_8_ = f32[16,16,128]{2,1,0:T(8,128)S(1)} collective-permute-done((f32[16,16,128]{2,1,0:T(8,128)S(1)}, f32[16,16,128]{2,1,0:T(8,128)S(1)}, u32[]{:S(2)}, u32[]{:S(2)}) %collective-permute-start.6) | collective-permute-done | bytes 131104 | tf_op jit(solution)/shard_map/ppermute | solution.py:29
  26.0 3.1 %second.1 = (f32[256,128]{1,0:T(8,128)}, f32[256,128]{1,0:T(8,128)}, f32[8,128]{1,0:T(8,128)S(1)}) custom-call(s32[4,32]{1,0:T(4,128)S(1)} %bitcast.8, f32[2]{0:T(128)S(1)} %copy-done.4, f32[32,128]{1,0:T(8,128)S(1)} %copy-done.1, f32[32,16,128]{2,1,0:T(8,128)S(1)} %get-tuple-element.22.refs_3_, f32[32,16,128]{2,1,0:T(8,128)S(1)} %get-tuple-element.23.refs_4_, ...), custom_call_target="tpu_custom_call" | custom-call | tf_op jit(solution)/shard_map/second/pallas_call | solution.py:247
  29.1 3.3 %collective-permute-start.10 = (f32[8,128]{1,0:T(8,128)S(1)}, f32[8,128]{1,0:T(8,128)S(1)}, u32[]{:S(2)}, u32[]{:S(2)}) collective-permute-start(f32[8,128]{1,0:T(8,128)S(1)} %get-tuple-element.30), channel_id=1, source_target_pairs={{0,128},{32,160},{64,192},{96,224},{128,0},{160,32},{192,64},{224,... | collective-permute-start | bytes 12296 | tf_op jit(solution)/shard_map/ppermute | solution.py:29
  32.4 1.1 %collective-permute-start.9 = (f32[8,128]{1,0:T(8,128)S(1)}, f32[8,128]{1,0:T(8,128)S(1)}, u32[]{:S(2)}, u32[]{:S(2)}) collective-permute-start(f32[8,128]{1,0:T(8,128)S(1)} %get-tuple-element.30), channel_id=1, source_target_pairs={{0,192},{32,224},{64,128},{96,160},{128,64},{160,96},{192,0},{224,... | collective-permute-start | bytes 12296 | tf_op jit(solution)/shard_map/ppermute | solution.py:29
  33.5 0.9 %collective-permute-done.10 = f32[8,128]{1,0:T(8,128)S(1)} collective-permute-done((f32[8,128]{1,0:T(8,128)S(1)}, f32[8,128]{1,0:T(8,128)S(1)}, u32[]{:S(2)}, u32[]{:S(2)}) %collective-permute-start.10) | collective-permute-done | bytes 4128 | tf_op jit(solution)/shard_map/ppermute | solution.py:29
  34.4 2.9 %collective-permute-done.9 = f32[8,128]{1,0:T(8,128)S(1)} collective-permute-done((f32[8,128]{1,0:T(8,128)S(1)}, f32[8,128]{1,0:T(8,128)S(1)}, u32[]{:S(2)}, u32[]{:S(2)}) %collective-permute-start.9) | collective-permute-done | bytes 4128 | tf_op jit(solution)/shard_map/ppermute | solution.py:29
  37.3 5.7 %collective-permute-start.11 = (f32[8,128]{1,0:T(8,128)S(1)}, f32[8,128]{1,0:T(8,128)S(1)}, u32[]{:S(2)}, u32[]{:S(2)}) collective-permute-start(f32[8,128]{1,0:T(8,128)S(1)} %add_add_fusion), channel_id=1, source_target_pairs={{0,32},{32,0},{64,96},{96,64},{128,160},{160,128},{192,224},{224,1... | collective-permute-start | bytes 12296 | tf_op jit(solution)/shard_map/ppermute | solution.py:29
  43.0 1.9 %collective-permute-done.11 = f32[8,128]{1,0:T(8,128)S(1)} collective-permute-done((f32[8,128]{1,0:T(8,128)S(1)}, f32[8,128]{1,0:T(8,128)S(1)}, u32[]{:S(2)}, u32[]{:S(2)}) %collective-permute-start.11) | collective-permute-done | bytes 4128 | tf_op jit(solution)/shard_map/ppermute | solution.py:29
  44.9 0.6 %bitcast_subtract_fusion = f32[1024]{0:T(1024)} fusion(f32[1024]{0:T(1024)S(1)} %copy-done.5, f32[8,128]{1,0:T(8,128)S(1)} %add_add_fusion, f32[8,128]{1,0:T(8,128)S(1)} %collective-permute-done.11), kind=kLoop, calls=%fused_computation | loop fusion | flops 6144 | bytes 16384 | tf_op jit(solution)/shard_map/sub | solution.py:264
  (18 shorter events, 0.0 us)
Async XLA Ops:
  1.8 10.6 %collective-permute-start = (f32[16,16,128]{2,1,0:T(8,128)S(1)}, f32[16,16,128]{2,1,0:T(8,128)S(1)}, u32[]{:S(2)}, u32[]{:S(2)}) collective-permute-start(f32[16,16,128]{2,1,0:T(8,128)S(1)} %get-tuple-element.18), channel_id=1, source_target_pairs={{0,1},{1,0},{2,3},{3,2},{4,5},{5,4},{6,7},{7,6},{8,9},{9,8},{10,11... | collective-permute-start | bytes 393224 | tf_op jit(solution)/shard_map/ppermute | solution.py:29
  1.9 10.5 %collective-permute-start.1 = (f32[16,16,128]{2,1,0:T(8,128)S(1)}, f32[16,16,128]{2,1,0:T(8,128)S(1)}, u32[]{:S(2)}, u32[]{:S(2)}) collective-permute-start(f32[16,16,128]{2,1,0:T(8,128)S(1)} %get-tuple-element.19), channel_id=1, source_target_pairs={{0,2},{1,3},{2,0},{3,1},{4,6},{5,7},{6,4},{7,5},{8,10},{9,11},{10,... | collective-permute-start | bytes 393224 | tf_op jit(solution)/shard_map/ppermute | solution.py:29
  3.9 9.9 %collective-permute-start.2 = (f32[16,16,128]{2,1,0:T(8,128)S(1)}, f32[16,16,128]{2,1,0:T(8,128)S(1)}, u32[]{:S(2)}, u32[]{:S(2)}) collective-permute-start(f32[16,16,128]{2,1,0:T(8,128)S(1)} %get-tuple-element.20), channel_id=1, source_target_pairs={{0,4},{1,5},{2,6},{3,7},{4,0},{5,1},{6,2},{7,3},{8,12},{9,13},{10,... | collective-permute-start | bytes 393224 | tf_op jit(solution)/shard_map/ppermute | solution.py:29
  7.2 6.6 %copy-start.1 = (f32[32,128]{1,0:T(8,128)S(1)}, f32[32,128]{1,0:T(8,128)}, u32[]{:S(2)}) copy-start(f32[32,128]{1,0:T(8,128)} %refs_2_.1) | copy-start | bytes 49156
  7.2 6.6 %copy-start.2 = (s32[4,16]{1,0:T(4,128)S(1)}, s32[4,16]{1,0:T(4,128)}, u32[]{:S(2)}) copy-start(s32[4,16]{1,0:T(4,128)} %tiles_ref.1) | copy-start | bytes 772
  7.2 6.6 %copy-start.3 = (s32[32,4]{0,1:T(4,128)S(1)}, s32[32,4]{0,1:T(4,128)}, u32[]{:S(2)}) copy-start(s32[32,4]{0,1:T(4,128)} %param.12) | copy-start | bytes 1540
  7.2 6.6 %copy-start.4 = (f32[2]{0:T(128)S(1)}, f32[2]{0:T(128)}, u32[]{:S(2)}) copy-start(f32[2]{0:T(128)} %refs_1_.1) | copy-start | bytes 28
  7.2 6.6 %collective-permute-start.3 = (f32[16,16,128]{2,1,0:T(8,128)S(1)}, f32[16,16,128]{2,1,0:T(8,128)S(1)}, u32[]{:S(2)}, u32[]{:S(2)}) collective-permute-start(f32[16,16,128]{2,1,0:T(8,128)S(1)} %get-tuple-element.21), channel_id=1, source_target_pairs={{0,8},{1,9},{2,10},{3,11},{4,12},{5,13},{6,14},{7,15},{8,0},{9,1},... | collective-permute-start | bytes 393224 | tf_op jit(solution)/shard_map/ppermute | solution.py:29
  12.4 13.6 %copy-start = (s32[12,1024]{1,0:T(8,128)S(1)}, s32[12,1024]{1,0:T(8,128)}, u32[]{:S(2)}) copy-start(s32[12,1024]{1,0:T(8,128)} %refs_10_.1) | copy-start | bytes 147460
  13.9 31.0 %copy-start.5 = (f32[1024]{0:T(1024)S(1)}, f32[1024]{0:T(1024)}, u32[]{:S(2)}) copy-start(f32[1024]{0:T(1024)} %param.17) | copy-start | bytes 12292
  16.2 4.3 %collective-permute-start.4 = (f32[16,16,128]{2,1,0:T(8,128)S(1)}, f32[16,16,128]{2,1,0:T(8,128)S(1)}, u32[]{:S(2)}, u32[]{:S(2)}) collective-permute-start(f32[16,16,128]{2,1,0:T(8,128)S(1)} %get-tuple-element.24), channel_id=1, source_target_pairs={{0,1},{1,0},{2,3},{3,2},{4,5},{5,4},{6,7},{7,6},{8,9},{9,8},{10,11... | collective-permute-start | bytes 393224 | tf_op jit(solution)/shard_map/ppermute | solution.py:29
  16.3 8.4 %collective-permute-start.5 = (f32[16,16,128]{2,1,0:T(8,128)S(1)}, f32[16,16,128]{2,1,0:T(8,128)S(1)}, u32[]{:S(2)}, u32[]{:S(2)}) collective-permute-start(f32[16,16,128]{2,1,0:T(8,128)S(1)} %get-tuple-element.25), channel_id=1, source_target_pairs={{0,2},{1,3},{2,0},{3,1},{4,6},{5,7},{6,4},{7,5},{8,10},{9,11},{10,... | collective-permute-start | bytes 393224 | tf_op jit(solution)/shard_map/ppermute | solution.py:29
  16.7 9.3 %collective-permute-start.6 = (f32[16,16,128]{2,1,0:T(8,128)S(1)}, f32[16,16,128]{2,1,0:T(8,128)S(1)}, u32[]{:S(2)}, u32[]{:S(2)}) collective-permute-start(f32[16,16,128]{2,1,0:T(8,128)S(1)} %get-tuple-element.26), channel_id=1, source_target_pairs={{0,4},{1,5},{2,6},{3,7},{4,0},{5,1},{6,2},{7,3},{8,12},{9,13},{10,... | collective-permute-start | bytes 393224 | tf_op jit(solution)/shard_map/ppermute | solution.py:29
  19.3 6.7 %collective-permute-start.7 = (f32[16,16,128]{2,1,0:T(8,128)S(1)}, f32[16,16,128]{2,1,0:T(8,128)S(1)}, u32[]{:S(2)}, u32[]{:S(2)}) collective-permute-start(f32[16,16,128]{2,1,0:T(8,128)S(1)} %get-tuple-element.27), channel_id=1, source_target_pairs={{0,8},{1,9},{2,10},{3,11},{4,12},{5,13},{6,14},{7,15},{8,0},{9,1},... | collective-permute-start | bytes 393224 | tf_op jit(solution)/shard_map/ppermute | solution.py:29
  29.1 5.2 %collective-permute-start.10 = (f32[8,128]{1,0:T(8,128)S(1)}, f32[8,128]{1,0:T(8,128)S(1)}, u32[]{:S(2)}, u32[]{:S(2)}) collective-permute-start(f32[8,128]{1,0:T(8,128)S(1)} %get-tuple-element.30), channel_id=1, source_target_pairs={{0,128},{32,160},{64,192},{96,224},{128,0},{160,32},{192,64},{224,... | collective-permute-start | bytes 12296 | tf_op jit(solution)/shard_map/ppermute | solution.py:29
  32.4 4.8 %collective-permute-start.9 = (f32[8,128]{1,0:T(8,128)S(1)}, f32[8,128]{1,0:T(8,128)S(1)}, u32[]{:S(2)}, u32[]{:S(2)}) collective-permute-start(f32[8,128]{1,0:T(8,128)S(1)} %get-tuple-element.30), channel_id=1, source_target_pairs={{0,192},{32,224},{64,128},{96,160},{128,64},{160,96},{192,0},{224,... | collective-permute-start | bytes 12296 | tf_op jit(solution)/shard_map/ppermute | solution.py:29
  33.5 3.8 %collective-permute-start.8 = (f32[8,128]{1,0:T(8,128)S(1)}, f32[8,128]{1,0:T(8,128)S(1)}, u32[]{:S(2)}, u32[]{:S(2)}) collective-permute-start(f32[8,128]{1,0:T(8,128)S(1)} %get-tuple-element.30), channel_id=1, source_target_pairs={{0,64},{32,96},{64,0},{96,32},{128,192},{160,224},{192,128},{224,1... | collective-permute-start | bytes 12296 | tf_op jit(solution)/shard_map/ppermute | solution.py:29
  37.3 7.6 %collective-permute-start.11 = (f32[8,128]{1,0:T(8,128)S(1)}, f32[8,128]{1,0:T(8,128)S(1)}, u32[]{:S(2)}, u32[]{:S(2)}) collective-permute-start(f32[8,128]{1,0:T(8,128)S(1)} %add_add_fusion), channel_id=1, source_target_pairs={{0,32},{32,0},{64,96},{96,64},{128,160},{160,128},{192,224},{224,1... | collective-permute-start | bytes 12296 | tf_op jit(solution)/shard_map/ppermute | solution.py:29

commit v3 on v2

--- a/solution.py
+++ b/solution.py
@@ -15,6 +15,8 @@
 RHO2 = 1.0 / (2.0 * SONE - RHO1)
 C1, C2 = RHO1 * RHO0, 2.0 * RHO1 / DELTA
 C3, C4 = RHO2 * RHO1, 2.0 * RHO2 / DELTA
+
+ORDER = (2, 1, 3, 0)
 
 F32, BF16 = jnp.float32, jnp.bfloat16
 VM = pl.BlockSpec(memory_space=pltpu.VMEM)
@@ -89,29 +91,17 @@
     pick(tiles_ref, field_ref, (send1, send2, send3, send4))
 
 
-def split(curl_ref, matrix_ref, buf, sems):
+def split(curl_ref, matrix_ref):
     blocks, links, width, _ = curl_ref.shape
-    groups = sems.shape[0]
-    per = blocks // groups
-    chunks = [pl.ds(g * per, per) for g in range(groups)]
-    copies = [
-        pltpu.make_async_copy(curl_ref.at[c], buf.at[c], sems.at[g]) for g, c in enumerate(chunks)
-    ]
-    for copy in copies:
-        copy.start()
-    for b in range(blocks):
-        if b % per == 0:
-            copies[b // per].wait()
+    for b in range(blocks):
         for k in range(links):
-            high, low = halves(buf[b, k])
+            high, low = halves(curl_ref[b, k])
             matrix_ref[b, k * width : (k + 1) * width, :width] = high.T
             matrix_ref[b, k * width : (k + 1) * width, width:] = low.T
 
 
-def extend(field_ref, got_refs, ext):
-    blocks, rows, _ = field_ref.shape
-    at = 0
-    for ref in (field_ref, *got_refs):
+def extend(rows, refs, ext, at=0):
+    for ref in refs:
         for t in range(ref.shape[0]):
             high, low = halves(ref[t])
             ext[at, :rows] = high
@@ -119,11 +109,21 @@
             at += 1
 
 
-def curl_row(b, links_ref, matrix_ref, ext):
-    rows, width = ext.shape[1] // 2, ext.shape[2]
-    x = jnp.concatenate([ext[links_ref[k, b]] for k in range(links_ref.shape[0])], axis=1)
-    y = jnp.dot(x, matrix_ref[b], preferred_element_type=F32)
+def by_round(got_refs):
+    got = dict(zip(ORDER, got_refs))
+    return [got[r] for r in range(len(ORDER))]
+
+
+def product(x, matrix):
+    rows, width = x.shape[0] // 2, matrix.shape[1] // 2
+    y = jnp.dot(x, matrix, preferred_element_type=F32)
     return y[:rows, :width] + (y[rows:, :width] + y[:rows, width:] + y[rows:, width:])
+
+
+def curl_row(b, links_ref, matrix_ref, ext, start=0):
+    links, width = links_ref.shape[0], ext.shape[2]
+    x = jnp.concatenate([ext[links_ref[k, b]] for k in range(start, links)], axis=1)
+    return product(x, matrix_ref[b, start * width :])
 
 
 def first(
@@ -131,7 +131,7 @@
     dir_ref, base_ref, send1, send2, send3, send4, ext,
 ):
     blocks, rows, lanes = field_ref.shape
-    extend(field_ref, (got1, got2, got3, got4), ext)
+    extend(rows, [field_ref] + by_round((got1, got2, got3, got4)), ext)
     omega, real = frequency_rows(omega_ref, rows, lanes)
     sign = jnp.where(real, -omega, omega)
     for b in range(blocks):
@@ -145,30 +145,35 @@
     pick(tiles_ref, dir_ref, (send1, send2, send3, send4))
 
 
-def second(
-    scale, links_ref, omega_ref, mass_ref, dir_ref, base_ref, matrix_ref, got1, got2, got3, got4,
-    cells_ref, fwd_hbm, adj_hbm, grad_ref, ext, table, fwd_ref, adj_ref, sems,
-):
+def middle(omega_ref, mass_ref, dir_ref, base_ref, matrix_ref, rest_ref, ext_ref):
     blocks, rows, lanes = dir_ref.shape
-    half = rows // 2
-    extend(dir_ref, (got1, got2, got3, got4), ext)
     omega, real = frequency_rows(omega_ref, rows, lanes)
     sign = jnp.where(real, -omega, omega)
     for b in range(blocks):
-        au = curl_row(b, links_ref, matrix_ref, ext)
-        au = au + sign * mass_ref[b : b + 1] * other(dir_ref[b])
-        x = base_ref[b] - C4 * au
+        u = dir_ref[b]
+        high, low = halves(u)
+        x = jnp.concatenate([high, low], axis=0)
+        ext_ref[b] = x
+        au = product(x, matrix_ref[b, :lanes]) + sign * mass_ref[b : b + 1] * other(u)
+        rest_ref[b] = base_ref[b] - C4 * au
+
+
+def second(
+    scale, links_ref, omega_ref, own_ref, rest_ref, matrix_ref, got1, got2, got3, got4,
+    cells_ref, fwd_ref, adj_ref, grad_ref, ext, table,
+):
+    blocks, rows, lanes = rest_ref.shape
+    half = rows // 2
+    ext[:blocks] = own_ref[...]
+    extend(rows, by_round((got1, got2, got3, got4)), ext, blocks)
+    omega, _ = frequency_rows(omega_ref, rows, lanes)
+    for b in range(blocks):
+        x = rest_ref[b] - C4 * curl_row(b, links_ref, matrix_ref, ext, 1)
         efield, lfield = x[:half], x[half:]
         fwd_ref[pl.ds(b, half, stride=blocks), :] = efield
         adj_ref[pl.ds(b, half, stride=blocks), :] = lfield
         prod = omega[:half] * efield * other(lfield)
         table[b : b + 1] = jnp.sum(prod, axis=0, keepdims=True)
-    copies = [
-        pltpu.make_async_copy(fwd_ref, fwd_hbm, sems.at[0]),
-        pltpu.make_async_copy(adj_ref, adj_hbm, sems.at[1]),
-    ]
-    for copy in copies:
-        copy.start()
     edges, cells = cells_ref.shape
     padded = -(-edges // 8) * 8
     for c in range(cells // lanes):
@@ -185,6 +190,13 @@
                 found = jnp.where(block == b, value, found)
             total = found if total is None else total + found
         grad_ref[c : c + 1] = jnp.sum(total, axis=0, keepdims=True) * scale
+
+
+def store(fwd_ref, adj_ref, fwd_hbm, adj_hbm, sems):
+    pairs = ((fwd_ref, fwd_hbm), (adj_ref, adj_hbm))
+    copies = [pltpu.make_async_copy(a, b, sems.at[i]) for i, (a, b) in enumerate(pairs)]
+    for copy in copies:
+        copy.start()
     for copy in copies:
         copy.wait()
 
@@ -212,26 +224,23 @@
         out_specs=[VM] * (1 + rounds),
         scratch_shapes=[pltpu.SMEM(tile_lists.shape, jnp.int32), flat_shape, flat_shape, DMA((3,))],
         compiler_params=params(8),
+        cost_estimate=cost(3 << 30, 1 << 20),
         name="prepare",
     )(far(tile_lists), far(fwd_source.reshape(flat)), far(adj_source.reshape(flat)))
 
     def trade(sends):
-        got = [None] * rounds
-        for r in (2, 1, 3, 0):
-            got[r] = swapped(sends[r], "dom", 2**r)
-        return [near(g) for g in got]
+        return [near(swapped(sends[r], "dom", 2**r)) for r in ORDER]
 
     got = trade(sends)
     matrix = pl.pallas_call(
         split,
         out_shape=matrix_shape,
-        in_specs=[HB],
+        in_specs=[VM],
         out_specs=VM,
-        scratch_shapes=[pltpu.VMEM(curl_blocks.shape, F32), DMA((blocks // 4,))],
         compiler_params=params(32),
         cost_estimate=cost(8 << 20, 16 << 20),
         name="split",
-    )(far(curl_blocks))
+    )(curl_blocks)
     matrix = near(matrix)
     direction, base, *sends = pl.pallas_call(
         first,
@@ -243,20 +252,39 @@
         name="first",
     )(links_t, tile_lists, omega, edge_mass, near(field), matrix, *got)
     got = trade(sends)
+    rest, own = pl.pallas_call(
+        middle,
+        out_shape=[field_shape, pltpu.VMEM((blocks, 2 * rows, lanes), BF16)],
+        in_specs=[SM] + [VM] * 4,
+        out_specs=[VM] * 2,
+        compiler_params=params(32),
+        cost_estimate=cost(1 << 20, 4 << 20),
+        name="middle",
+    )(omega, edge_mass, near(direction), near(base), matrix)
     scale = 1.0 / math.sqrt(24.0 * count * lax.axis_size("freq"))
     efield, lfield, grad = pl.pallas_call(
         lambda *refs: second(scale, *refs),
         out_shape=[
-            pltpu.HBM(flat, F32),
-            pltpu.HBM(flat, F32),
+            flat_shape,
+            flat_shape,
             pltpu.VMEM((log_cond.shape[0] // lanes, lanes), F32),
         ],
-        in_specs=[SM] * 2 + [VM] * (5 + rounds),
-        out_specs=[HB, HB, VM],
-        scratch_shapes=[ext, pltpu.VMEM((blocks, lanes), F32), flat_shape, flat_shape, DMA((2,))],
+        in_specs=[SM] * 2 + [VM] * (4 + rounds),
+        out_specs=[VM] * 3,
+        scratch_shapes=[ext, pltpu.VMEM((blocks, lanes), F32)],
         compiler_params=params(32),
         name="second",
-    )(links_t, omega, edge_mass, near(direction), near(base), matrix, *got, cell_edges)
+    )(links_t, omega, near(own), near(rest), matrix, *got, cell_edges)
+    efield, lfield = pl.pallas_call(
+        store,
+        out_shape=[pltpu.HBM(flat, F32)] * 2,
+        in_specs=[VM] * 2,
+        out_specs=[HB] * 2,
+        scratch_shapes=[DMA((2,))],
+        compiler_params=params(8),
+        cost_estimate=cost(1 << 10, 1 << 20),
+        name="store",
+    )(near(efield), near(lfield))
     got = [swapped(grad, "freq", mask) for mask in (2, 6, 4)]
     grad = grad + got[0] + got[1] + got[2]
     grad = grad + swapped(grad, "freq", 1)

time: 45.6 us -> 41.8 us (0.917)
  waiting for transfers between devices: 12.5 us -> 9.02 us
  Pallas kernels: 10.5 us -> 9.77 us
  starting transfers between devices: 21 us -> 21.6 us
    ppermute x12, waiting for transfers between devices: 12.5 us -> 9.02 us  [swapped(): return lax.ppermute(value, axis, pairs)]
    pallas_call x2 -> x4, Pallas kernels: 7.03 us -> 6.12 us  [the longest x1 2.22 us: local(): pl.pallas_call(lambda *refs: second(scale, *refs), out_shape=[flat_shape,...]
    ppermute x12, starting transfers between devices: 21 us -> 21.6 us  [swapped(): return lax.ppermute(value, axis, pairs)]
  transfers between devices with their start and end apart: 12 -> 12, of which waited for: 6 -> 9; matrix products, arithmetic and copies ran while one was open for 0% -> 0% of each run, Pallas kernels for 9% -> 9%
where the time goes in v3:
time: 41.8 us; the launch traced here: 41.7 us
  starting transfers between devices  21.6 us (52%)
  Pallas kernels  9.77 us (23%)
  waiting for transfers between devices  9.02 us (22%)
  between operations  0.74 us (2%)
  other arithmetic  0.61 us (1%)
    ppermute x12, starting transfers between devices, swapped(): return lax.ppermute(value, axis, pairs)  21.6 us
    ppermute x12, waiting for transfers between devices, swapped(): return lax.ppermute(value, axis, pairs)  9.02 us
    pallas_call x1, Pallas kernels, local(): pl.pallas_call(first, out_shape=[field_shape] * 2 + [tile_shape] * rounds...  2.3 us
    pallas_call x1, Pallas kernels, local(): pl.pallas_call(lambda *refs: second(scale, *refs), out_shape=[flat_shape,...  2.22 us
    pallas_call x1, Pallas kernels, local(): pl.pallas_call(split, out_shape=matrix_shape, in_specs=[VM], out_specs=VM...  2.21 us
    pallas_call x1, Pallas kernels, local(): pl.pallas_call(prepare, out_shape=[field_shape] + [tile_shape] * rounds,...  1.34 us
    pallas_call x1, Pallas kernels, local(): pl.pallas_call(middle, out_shape=[field_shape, pltpu.VMEM((blocks, 2 * ro...  0.98 us
  transfers between devices with their start and end apart: 12, of which 9 were waited for; matrix products, arithmetic and copies ran while one was open for 0% of the time, Pallas kernels for 9%

profile of v3, /device:TPU:4, one launch (start us, length us, event | category | flops | bytes accessed | tf_op | source)
XLA Modules:
  0.0 41.7 jit_solution(16746157631141078645)
XLA Ops:
  0.6 1.3 %prepare.1 = (f32[32,16,128]{2,1,0:T(8,128)S(1)}, f32[16,16,128]{2,1,0:T(8,128)S(1)}, f32[16,16,128]{2,1,0:T(8,128)S(1)}, f32[16,16,128]{2,1,0:T(8,128)S(1)}, f32[16,16,128]{2,1,0:T(8,128)S(1)}) custom-call(s32[4,16]{1,0:T(4,128)} %tiles_ref.1, f32[256,128]{1,0:T(8,128)} %bitcast.9, f32[256,128]{1,0:T(8,128)} %bitcast.10), custom_call_target="tpu_custom_call" | custom-call | flops 3221225472 | bytes 1048576 | tf_op jit(solution)/shard_map/prepare/pallas_call | solution.py:220
  2.0 3.4 %collective-permute-start = (f32[16,16,128]{2,1,0:T(8,128)S(1)}, f32[16,16,128]{2,1,0:T(8,128)S(1)}, u32[]{:S(2)}, u32[]{:S(2)}) collective-permute-start(f32[16,16,128]{2,1,0:T(8,128)S(1)} %get-tuple-element.22), channel_id=1, source_target_pairs={{0,4},{1,5},{2,6},{3,7},{4,0},{5,1},{6,2},{7,3},{8,12},{9,13},{10,... | collective-permute-start | bytes 393224 | tf_op jit(solution)/shard_map/ppermute | solution.py:31
  5.4 1.9 %collective-permute-start.1 = (f32[16,16,128]{2,1,0:T(8,128)S(1)}, f32[16,16,128]{2,1,0:T(8,128)S(1)}, u32[]{:S(2)}, u32[]{:S(2)}) collective-permute-start(f32[16,16,128]{2,1,0:T(8,128)S(1)} %get-tuple-element.23), channel_id=1, source_target_pairs={{0,2},{1,3},{2,0},{3,1},{4,6},{5,7},{6,4},{7,5},{8,10},{9,11},{10,... | collective-permute-start | bytes 393224 | tf_op jit(solution)/shard_map/ppermute | solution.py:31
  7.3 1.2 %collective-permute-start.2 = (f32[16,16,128]{2,1,0:T(8,128)S(1)}, f32[16,16,128]{2,1,0:T(8,128)S(1)}, u32[]{:S(2)}, u32[]{:S(2)}) collective-permute-start(f32[16,16,128]{2,1,0:T(8,128)S(1)} %get-tuple-element.24), channel_id=1, source_target_pairs={{0,8},{1,9},{2,10},{3,11},{4,12},{5,13},{6,14},{7,15},{8,0},{9,1},... | collective-permute-start | bytes 393224 | tf_op jit(solution)/shard_map/ppermute | solution.py:31
  8.5 0.1 collective-permute-start.3
  8.6 2.2 %split.1.matrix_ref.refs_4_ = bf16[32,512,256]{2,1,0:T(8,128)(2,1)S(1)} custom-call(f32[32,4,128,128]{3,2,1,0:T(8,128)S(1)} %copy-done), custom_call_target="tpu_custom_call" | custom-call | flops 8388608 | bytes 16777216 | tf_op jit(solution)/shard_map/split/pallas_call | solution.py:235
  10.8 1.0 %collective-permute-done.got1 = f32[16,16,128]{2,1,0:T(8,128)S(1)} collective-permute-done((f32[16,16,128]{2,1,0:T(8,128)S(1)}, f32[16,16,128]{2,1,0:T(8,128)S(1)}, u32[]{:S(2)}, u32[]{:S(2)}) %collective-permute-start) | collective-permute-done | bytes 131104 | tf_op jit(solution)/shard_map/ppermute | solution.py:31
  11.8 0.4 collective-permute-done.2.got3
  12.3 2.3 %first.1 = (f32[32,16,128]{2,1,0:T(8,128)S(1)}, f32[32,16,128]{2,1,0:T(8,128)S(1)}, f32[16,16,128]{2,1,0:T(8,128)S(1)}, f32[16,16,128]{2,1,0:T(8,128)S(1)}, f32[...) custom-call(s32[4,32]{1,0:T(4,128)S(1)} %bitcast.7, s32[4,16]{1,0:T(4,128)S(1)} %copy-done.5, f32[2]{0:T(128)S(1)} %copy-done.4, ...), custom_call_target="tpu_custom_call" | custom-call | tf_op jit(solution)/shard_map/first/pallas_call | solution.py:245
  14.6 1.5 %collective-permute-start.4 = (f32[16,16,128]{2,1,0:T(8,128)S(1)}, f32[16,16,128]{2,1,0:T(8,128)S(1)}, u32[]{:S(2)}, u32[]{:S(2)}) collective-permute-start(f32[16,16,128]{2,1,0:T(8,128)S(1)} %get-tuple-element.30), channel_id=1, source_target_pairs={{0,4},{1,5},{2,6},{3,7},{4,0},{5,1},{6,2},{7,3},{8,12},{9,13},{10,... | collective-permute-start | bytes 393224 | tf_op jit(solution)/shard_map/ppermute | solution.py:31
  16.1 2.2 %collective-permute-start.5 = (f32[16,16,128]{2,1,0:T(8,128)S(1)}, f32[16,16,128]{2,1,0:T(8,128)S(1)}, u32[]{:S(2)}, u32[]{:S(2)}) collective-permute-start(f32[16,16,128]{2,1,0:T(8,128)S(1)} %get-tuple-element.31), channel_id=1, source_target_pairs={{0,2},{1,3},{2,0},{3,1},{4,6},{5,7},{6,4},{7,5},{8,10},{9,11},{10,... | collective-permute-start | bytes 393224 | tf_op jit(solution)/shard_map/ppermute | solution.py:31
  18.2 1.2 %collective-permute-start.6 = (f32[16,16,128]{2,1,0:T(8,128)S(1)}, f32[16,16,128]{2,1,0:T(8,128)S(1)}, u32[]{:S(2)}, u32[]{:S(2)}) collective-permute-start(f32[16,16,128]{2,1,0:T(8,128)S(1)} %get-tuple-element.32), channel_id=1, source_target_pairs={{0,8},{1,9},{2,10},{3,11},{4,12},{5,13},{6,14},{7,15},{8,0},{9,1},... | collective-permute-start | bytes 393224 | tf_op jit(solution)/shard_map/ppermute | solution.py:31
  19.4 1.0 %middle.1 = (f32[32,16,128]{2,1,0:T(8,128)S(1)}, bf16[32,32,128]{2,1,0:T(8,128)(2,1)S(1)}) custom-call(f32[2]{0:T(128)S(1)} %copy-done.4, f32[32,128]{1,0:T(8,128)S(1)} %copy-done.2, f32[32,16,128]{2,1,0:T(8,128)S(1)} %get-tuple-element.26.dir_ref, f32[32,16,128]{2,1,0:T(8,128)S(1)} %get-tuple-element.27.base_ref, ...), custom_call_target="tpu_custom_call" | custom-call | flops 1048576 | bytes 4194304 | tf_op jit(solution)/shard_map/middle/pallas_call | solution.py:255
  20.4 2.6 %collective-permute-done.4.refs_5_ = f32[16,16,128]{2,1,0:T(8,128)S(1)} collective-permute-done((f32[16,16,128]{2,1,0:T(8,128)S(1)}, f32[16,16,128]{2,1,0:T(8,128)S(1)}, u32[]{:S(2)}, u32[]{:S(2)}) %collective-permute-start.4) | collective-permute-done | bytes 131104 | tf_op jit(solution)/shard_map/ppermute | solution.py:31
  23.1 0.1 collective-permute-done.6.refs_7_
  23.2 2.2 %second.1 = (f32[256,128]{1,0:T(8,128)S(1)}, f32[256,128]{1,0:T(8,128)S(1)}, f32[8,128]{1,0:T(8,128)S(1)}) custom-call(s32[4,32]{1,0:T(4,128)S(1)} %bitcast.8, f32[2]{0:T(128)S(1)} %copy-done.4, bf16[32,32,128]{2,1,0:T(8,128)(2,1)S(1)} %get-tuple-element.28.refs_2_, f32[32,16,128]{2,1,0:T(8,128)S(1)} %get-tuple-element.29.refs_3_, ...), custom_call_target="tpu_custom_call" | custom-call | tf_op jit(solution)/shard_map/second/pallas_call | solution.py:265
  25.4 3.3 %collective-permute-start.10 = (f32[8,128]{1,0:T(8,128)S(1)}, f32[8,128]{1,0:T(8,128)S(1)}, u32[]{:S(2)}, u32[]{:S(2)}) collective-permute-start(f32[8,128]{1,0:T(8,128)S(1)} %get-tuple-element.38), channel_id=1, source_target_pairs={{0,128},{32,160},{64,192},{96,224},{128,0},{160,32},{192,64},{224,... | collective-permute-start | bytes 12296 | tf_op jit(solution)/shard_map/ppermute | solution.py:31
  28.7 1.1 %collective-permute-start.9 = (f32[8,128]{1,0:T(8,128)S(1)}, f32[8,128]{1,0:T(8,128)S(1)}, u32[]{:S(2)}, u32[]{:S(2)}) collective-permute-start(f32[8,128]{1,0:T(8,128)S(1)} %get-tuple-element.38), channel_id=1, source_target_pairs={{0,192},{32,224},{64,128},{96,160},{128,64},{160,96},{192,0},{224,... | collective-permute-start | bytes 12296 | tf_op jit(solution)/shard_map/ppermute | solution.py:31
  29.8 0.9 %collective-permute-done.10 = f32[8,128]{1,0:T(8,128)S(1)} collective-permute-done((f32[8,128]{1,0:T(8,128)S(1)}, f32[8,128]{1,0:T(8,128)S(1)}, u32[]{:S(2)}, u32[]{:S(2)}) %collective-permute-start.10) | collective-permute-done | bytes 4128 | tf_op jit(solution)/shard_map/ppermute | solution.py:31
  30.6 2.9 %collective-permute-done.9 = f32[8,128]{1,0:T(8,128)S(1)} collective-permute-done((f32[8,128]{1,0:T(8,128)S(1)}, f32[8,128]{1,0:T(8,128)S(1)}, u32[]{:S(2)}, u32[]{:S(2)}) %collective-permute-start.9) | collective-permute-done | bytes 4128 | tf_op jit(solution)/shard_map/ppermute | solution.py:31
  33.5 5.8 %collective-permute-start.11 = (f32[8,128]{1,0:T(8,128)S(1)}, f32[8,128]{1,0:T(8,128)S(1)}, u32[]{:S(2)}, u32[]{:S(2)}) collective-permute-start(f32[8,128]{1,0:T(8,128)S(1)} %add_add_fusion), channel_id=1, source_target_pairs={{0,32},{32,0},{64,96},{96,64},{128,160},{160,128},{192,224},{224,1... | collective-permute-start | bytes 12296 | tf_op jit(solution)/shard_map/ppermute | solution.py:31
  39.3 0.7 %store.1 = (f32[256,128]{1,0:T(8,128)}, f32[256,128]{1,0:T(8,128)}) custom-call(f32[256,128]{1,0:T(8,128)S(1)} %get-tuple-element.34.fwd_ref, f32[256,128]{1,0:T(8,128)S(1)} %get-tuple-element.35.adj_ref), custom_call_target="tpu_custom_call" | custom-call | flops 1024 | bytes 1048576 | tf_op jit(solution)/shard_map/store/pallas_call | solution.py:278
  40.1 1.1 %collective-permute-done.11 = f32[8,128]{1,0:T(8,128)S(1)} collective-permute-done((f32[8,128]{1,0:T(8,128)S(1)}, f32[8,128]{1,0:T(8,128)S(1)}, u32[]{:S(2)}, u32[]{:S(2)}) %collective-permute-start.11) | collective-permute-done | bytes 4128 | tf_op jit(solution)/shard_map/ppermute | solution.py:31
  41.1 0.6 %bitcast_subtract_fusion = f32[1024]{0:T(1024)} fusion(f32[1024]{0:T(1024)S(1)} %copy-done.6, f32[8,128]{1,0:T(8,128)S(1)} %add_add_fusion, f32[8,128]{1,0:T(8,128)S(1)} %collective-permute-done.11), kind=kLoop, calls=%fused_computation | loop fusion | flops 6144 | bytes 16384 | tf_op jit(solution)/shard_map/sub | solution.py:292
  (22 shorter events, 0.2 us)
Async XLA Ops:
  0.6 8.0 %copy-start = (f32[32,4,128,128]{3,2,1,0:T(8,128)S(1)}, f32[32,4,128,128]{3,2,1,0:T(8,128)}, u32[]{:S(2)}) copy-start(f32[32,4,128,128]{3,2,1,0:T(8,128)} %curl_ref.1) | copy-start | bytes 25165828
  2.0 9.8 %collective-permute-start = (f32[16,16,128]{2,1,0:T(8,128)S(1)}, f32[16,16,128]{2,1,0:T(8,128)S(1)}, u32[]{:S(2)}, u32[]{:S(2)}) collective-permute-start(f32[16,16,128]{2,1,0:T(8,128)S(1)} %get-tuple-element.22), channel_id=1, source_target_pairs={{0,4},{1,5},{2,6},{3,7},{4,0},{5,1},{6,2},{7,3},{8,12},{9,13},{10,... | collective-permute-start | bytes 393224 | tf_op jit(solution)/shard_map/ppermute | solution.py:31
  5.4 6.5 %collective-permute-start.1 = (f32[16,16,128]{2,1,0:T(8,128)S(1)}, f32[16,16,128]{2,1,0:T(8,128)S(1)}, u32[]{:S(2)}, u32[]{:S(2)}) collective-permute-start(f32[16,16,128]{2,1,0:T(8,128)S(1)} %get-tuple-element.23), channel_id=1, source_target_pairs={{0,2},{1,3},{2,0},{3,1},{4,6},{5,7},{6,4},{7,5},{8,10},{9,11},{10,... | collective-permute-start | bytes 393224 | tf_op jit(solution)/shard_map/ppermute | solution.py:31
  7.3 5.0 %collective-permute-start.2 = (f32[16,16,128]{2,1,0:T(8,128)S(1)}, f32[16,16,128]{2,1,0:T(8,128)S(1)}, u32[]{:S(2)}, u32[]{:S(2)}) collective-permute-start(f32[16,16,128]{2,1,0:T(8,128)S(1)} %get-tuple-element.24), channel_id=1, source_target_pairs={{0,8},{1,9},{2,10},{3,11},{4,12},{5,13},{6,14},{7,15},{8,0},{9,1},... | collective-permute-start | bytes 393224 | tf_op jit(solution)/shard_map/ppermute | solution.py:31
  8.5 3.8 %copy-start.2 = (f32[32,128]{1,0:T(8,128)S(1)}, f32[32,128]{1,0:T(8,128)}, u32[]{:S(2)}) copy-start(f32[32,128]{1,0:T(8,128)} %mass_ref.3) | copy-start | bytes 49156
  8.5 3.8 %copy-start.3 = (s32[32,4]{0,1:T(4,128)S(1)}, s32[32,4]{0,1:T(4,128)}, u32[]{:S(2)}) copy-start(s32[32,4]{0,1:T(4,128)} %param.12) | copy-start | bytes 1540
  8.5 3.8 %copy-start.4 = (f32[2]{0:T(128)S(1)}, f32[2]{0:T(128)}, u32[]{:S(2)}) copy-start(f32[2]{0:T(128)} %refs_1_.1) | copy-start | bytes 28
  8.5 3.8 %copy-start.5 = (s32[4,16]{1,0:T(4,128)S(1)}, s32[4,16]{1,0:T(4,128)}, u32[]{:S(2)}) copy-start(s32[4,16]{1,0:T(4,128)} %tiles_ref.1) | copy-start | bytes 772
  8.5 3.8 %collective-permute-start.3 = (f32[16,16,128]{2,1,0:T(8,128)S(1)}, f32[16,16,128]{2,1,0:T(8,128)S(1)}, u32[]{:S(2)}, u32[]{:S(2)}) collective-permute-start(f32[16,16,128]{2,1,0:T(8,128)S(1)} %get-tuple-element.25), channel_id=1, source_target_pairs={{0,1},{1,0},{2,3},{3,2},{4,5},{5,4},{6,7},{7,6},{8,9},{9,8},{10,11... | collective-permute-start | bytes 393224 | tf_op jit(solution)/shard_map/ppermute | solution.py:31
  12.3 10.9 %copy-start.1 = (s32[12,1024]{1,0:T(8,128)S(1)}, s32[12,1024]{1,0:T(8,128)}, u32[]{:S(2)}) copy-start(s32[12,1024]{1,0:T(8,128)} %refs_9_.1) | copy-start | bytes 147460
  14.6 8.4 %collective-permute-start.4 = (f32[16,16,128]{2,1,0:T(8,128)S(1)}, f32[16,16,128]{2,1,0:T(8,128)S(1)}, u32[]{:S(2)}, u32[]{:S(2)}) collective-permute-start(f32[16,16,128]{2,1,0:T(8,128)S(1)} %get-tuple-element.30), channel_id=1, source_target_pairs={{0,4},{1,5},{2,6},{3,7},{4,0},{5,1},{6,2},{7,3},{8,12},{9,13},{10,... | collective-permute-start | bytes 393224 | tf_op jit(solution)/shard_map/ppermute | solution.py:31
  16.1 7.0 %collective-permute-start.5 = (f32[16,16,128]{2,1,0:T(8,128)S(1)}, f32[16,16,128]{2,1,0:T(8,128)S(1)}, u32[]{:S(2)}, u32[]{:S(2)}) collective-permute-start(f32[16,16,128]{2,1,0:T(8,128)S(1)} %get-tuple-element.31), channel_id=1, source_target_pairs={{0,2},{1,3},{2,0},{3,1},{4,6},{5,7},{6,4},{7,5},{8,10},{9,11},{10,... | collective-permute-start | bytes 393224 | tf_op jit(solution)/shard_map/ppermute | solution.py:31
  18.2 5.0 %collective-permute-start.6 = (f32[16,16,128]{2,1,0:T(8,128)S(1)}, f32[16,16,128]{2,1,0:T(8,128)S(1)}, u32[]{:S(2)}, u32[]{:S(2)}) collective-permute-start(f32[16,16,128]{2,1,0:T(8,128)S(1)} %get-tuple-element.32), channel_id=1, source_target_pairs={{0,8},{1,9},{2,10},{3,11},{4,12},{5,13},{6,14},{7,15},{8,0},{9,1},... | collective-permute-start | bytes 393224 | tf_op jit(solution)/shard_map/ppermute | solution.py:31
  19.4 3.8 %collective-permute-start.7 = (f32[16,16,128]{2,1,0:T(8,128)S(1)}, f32[16,16,128]{2,1,0:T(8,128)S(1)}, u32[]{:S(2)}, u32[]{:S(2)}) collective-permute-start(f32[16,16,128]{2,1,0:T(8,128)S(1)} %get-tuple-element.33), channel_id=1, source_target_pairs={{0,1},{1,0},{2,3},{3,2},{4,5},{5,4},{6,7},{7,6},{8,9},{9,8},{10,11... | collective-permute-start | bytes 393224 | tf_op jit(solution)/shard_map/ppermute | solution.py:31
  19.4 21.7 %copy-start.6 = (f32[1024]{0:T(1024)S(1)}, f32[1024]{0:T(1024)}, u32[]{:S(2)}) copy-start(f32[1024]{0:T(1024)} %param.17) | copy-start | bytes 12292
  25.4 5.2 %collective-permute-start.10 = (f32[8,128]{1,0:T(8,128)S(1)}, f32[8,128]{1,0:T(8,128)S(1)}, u32[]{:S(2)}, u32[]{:S(2)}) collective-permute-start(f32[8,128]{1,0:T(8,128)S(1)} %get-tuple-element.38), channel_id=1, source_target_pairs={{0,128},{32,160},{64,192},{96,224},{128,0},{160,32},{192,64},{224,... | collective-permute-start | bytes 12296 | tf_op jit(solution)/shard_map/ppermute | solution.py:31
  28.7 4.8 %collective-permute-start.9 = (f32[8,128]{1,0:T(8,128)S(1)}, f32[8,128]{1,0:T(8,128)S(1)}, u32[]{:S(2)}, u32[]{:S(2)}) collective-permute-start(f32[8,128]{1,0:T(8,128)S(1)} %get-tuple-element.38), channel_id=1, source_target_pairs={{0,192},{32,224},{64,128},{96,160},{128,64},{160,96},{192,0},{224,... | collective-permute-start | bytes 12296 | tf_op jit(solution)/shard_map/ppermute | solution.py:31
  29.7 3.8 %collective-permute-start.8 = (f32[8,128]{1,0:T(8,128)S(1)}, f32[8,128]{1,0:T(8,128)S(1)}, u32[]{:S(2)}, u32[]{:S(2)}) collective-permute-start(f32[8,128]{1,0:T(8,128)S(1)} %get-tuple-element.38), channel_id=1, source_target_pairs={{0,64},{32,96},{64,0},{96,32},{128,192},{160,224},{192,128},{224,1... | collective-permute-start | bytes 12296 | tf_op jit(solution)/shard_map/ppermute | solution.py:31
  33.5 7.6 %collective-permute-start.11 = (f32[8,128]{1,0:T(8,128)S(1)}, f32[8,128]{1,0:T(8,128)S(1)}, u32[]{:S(2)}, u32[]{:S(2)}) collective-permute-start(f32[8,128]{1,0:T(8,128)S(1)} %add_add_fusion), channel_id=1, source_target_pairs={{0,32},{32,0},{64,96},{96,64},{128,160},{160,128},{192,224},{224,1... | collective-permute-start | bytes 12296 | tf_op jit(solution)/shard_map/ppermute | solution.py:31

commit v4 on v3

--- a/solution.py
+++ b/solution.py
@@ -91,13 +91,17 @@
     pick(tiles_ref, field_ref, (send1, send2, send3, send4))
 
 
-def split(curl_ref, matrix_ref):
+def split(omega_ref, mass_ref, field_ref, curl_ref, matrix_ref, rest_ref, ext_ref):
     blocks, links, width, _ = curl_ref.shape
+    rows, lanes = field_ref.shape[1:]
+    sign = signs(omega_ref, rows, lanes)
     for b in range(blocks):
         for k in range(links):
             high, low = halves(curl_ref[b, k])
-            matrix_ref[b, k * width : (k + 1) * width, :width] = high.T
-            matrix_ref[b, k * width : (k + 1) * width, width:] = low.T
+            both = jnp.concatenate([high.T, low.T], axis=1)
+            matrix_ref[b, k * width : (k + 1) * width] = both
+            if k == 0:
+                own_row(b, 1.0, sign, both, mass_ref, field_ref, field_ref, rest_ref, ext_ref)
 
 
 def extend(rows, refs, ext, at=0):
@@ -126,36 +130,41 @@
     return product(x, matrix_ref[b, start * width :])
 
 
+def signs(omega_ref, rows, lanes):
+    omega, real = frequency_rows(omega_ref, rows, lanes)
+    return jnp.where(real, -omega, omega)
+
+
+def own_row(b, scale, sign, matrix, mass_ref, field_ref, start_ref, rest_ref, ext_ref):
+    u = field_ref[b]
+    x = jnp.concatenate(halves(u), axis=0)
+    ext_ref[b] = x
+    au = product(x, matrix) + sign * mass_ref[b : b + 1] * other(u)
+    rest_ref[b] = start_ref[b] - scale * au
+
+
+def middle(scale, omega_ref, mass_ref, field_ref, start_ref, matrix_ref, rest_ref, ext_ref):
+    blocks, rows, lanes = field_ref.shape
+    sign = signs(omega_ref, rows, lanes)
+    for b in range(blocks):
+        own_row(
+            b, scale, sign, matrix_ref[b, :lanes], mass_ref, field_ref, start_ref, rest_ref, ext_ref
+        )
+
+
 def first(
-    links_ref, tiles_ref, omega_ref, mass_ref, field_ref, matrix_ref, got1, got2, got3, got4,
+    links_ref, tiles_ref, field_ref, own_ref, rest_ref, matrix_ref, got1, got2, got3, got4,
     dir_ref, base_ref, send1, send2, send3, send4, ext,
 ):
-    blocks, rows, lanes = field_ref.shape
-    extend(rows, [field_ref] + by_round((got1, got2, got3, got4)), ext)
-    omega, real = frequency_rows(omega_ref, rows, lanes)
-    sign = jnp.where(real, -omega, omega)
-    for b in range(blocks):
-        u = field_ref[b]
-        au = curl_row(b, links_ref, matrix_ref, ext)
-        au = au + sign * mass_ref[b : b + 1] * other(u)
-        resid = u - au
-        direction = C1 * u + C2 * resid
+    blocks, rows, _ = field_ref.shape
+    ext[:blocks] = own_ref[...]
+    extend(rows, by_round((got1, got2, got3, got4)), ext, blocks)
+    for b in range(blocks):
+        resid = rest_ref[b] - curl_row(b, links_ref, matrix_ref, ext, 1)
+        direction = C1 * field_ref[b] + C2 * resid
         dir_ref[b] = direction
-        base_ref[b] = u + direction + C3 * direction + C4 * resid
+        base_ref[b] = field_ref[b] + direction + C3 * direction + C4 * resid
     pick(tiles_ref, dir_ref, (send1, send2, send3, send4))
-
-
-def middle(omega_ref, mass_ref, dir_ref, base_ref, matrix_ref, rest_ref, ext_ref):
-    blocks, rows, lanes = dir_ref.shape
-    omega, real = frequency_rows(omega_ref, rows, lanes)
-    sign = jnp.where(real, -omega, omega)
-    for b in range(blocks):
-        u = dir_ref[b]
-        high, low = halves(u)
-        x = jnp.concatenate([high, low], axis=0)
-        ext_ref[b] = x
-        au = product(x, matrix_ref[b, :lanes]) + sign * mass_ref[b : b + 1] * other(u)
-        rest_ref[b] = base_ref[b] - C4 * au
 
 
 def second(
@@ -175,21 +184,25 @@
         prod = omega[:half] * efield * other(lfield)
         table[b : b + 1] = jnp.sum(prod, axis=0, keepdims=True)
     edges, cells = cells_ref.shape
-    padded = -(-edges // 8) * 8
-    for c in range(cells // lanes):
-        index = cells_ref[:, c * lanes : (c + 1) * lanes]
-        fill = jnp.full((padded - edges, lanes), -1, jnp.int32)
-        index = jnp.concatenate([index, fill], axis=0)
-        total = None
-        for e in range(0, padded, 8):
-            block, lane = index[e : e + 8] >> 7, index[e : e + 8] & 127
-            found = jnp.zeros((8, lanes), F32)
-            for b in range(blocks):
-                row = jnp.broadcast_to(table[b : b + 1], (8, lanes))
-                value = jnp.take_along_axis(row, lane, axis=1, mode="promise_in_bounds")
-                found = jnp.where(block == b, value, found)
-            total = found if total is None else total + found
-        grad_ref[c : c + 1] = jnp.sum(total, axis=0, keepdims=True) * scale
+
+    def find(index):
+        block, lane = index >> 7, index & 127
+        found = jnp.zeros(index.shape, F32)
+        for b in range(blocks):
+            row = jnp.broadcast_to(table[b : b + 1], index.shape)
+            value = jnp.take_along_axis(row, lane, axis=1, mode="promise_in_bounds")
+            found = jnp.where(block == b, value, found)
+        return found
+
+    def total(found):
+        return jnp.sum(found, axis=0, keepdims=True)
+
+    for c in range(0, cells // lanes, 2):
+        left = cells_ref[:, c * lanes : (c + 1) * lanes]
+        right = cells_ref[:, (c + 1) * lanes : (c + 2) * lanes]
+        last = find(jnp.concatenate([left[8:], right[8:]], axis=0))
+        grad_ref[c : c + 1] = (total(find(left[:8])) + total(last[: edges - 8])) * scale
+        grad_ref[c + 1 : c + 2] = (total(find(right[:8])) + total(last[edges - 8 :])) * scale
 
 
 def store(fwd_ref, adj_ref, fwd_hbm, adj_hbm, sems):
@@ -232,35 +245,42 @@
         return [near(swapped(sends[r], "dom", 2**r)) for r in ORDER]
 
     got = trade(sends)
-    matrix = pl.pallas_call(
-        split,
-        out_shape=matrix_shape,
-        in_specs=[VM],
-        out_specs=VM,
-        compiler_params=params(32),
-        cost_estimate=cost(8 << 20, 16 << 20),
-        name="split",
-    )(curl_blocks)
-    matrix = near(matrix)
+    own_shape = pltpu.VMEM((blocks, 2 * rows, lanes), BF16)
+    field = near(field)
+    matrix, rest, own = [
+        near(out)
+        for out in pl.pallas_call(
+            split,
+            out_shape=[matrix_shape, field_shape, own_shape],
+            in_specs=[SM] + [VM] * 3,
+            out_specs=[VM] * 3,
+            compiler_params=params(32),
+            cost_estimate=cost(8 << 20, 16 << 20),
+            name="split",
+        )(omega, edge_mass, field, curl_blocks)
+    ]
     direction, base, *sends = pl.pallas_call(
         first,
         out_shape=[field_shape] * 2 + [tile_shape] * rounds,
-        in_specs=[SM] * 3 + [VM] * (3 + rounds),
+        in_specs=[SM] * 2 + [VM] * (4 + rounds),
         out_specs=[VM] * (2 + rounds),
         scratch_shapes=[ext],
         compiler_params=params(32),
         name="first",
-    )(links_t, tile_lists, omega, edge_mass, near(field), matrix, *got)
+    )(links_t, tile_lists, field, own, rest, matrix, *got)
     got = trade(sends)
-    rest, own = pl.pallas_call(
-        middle,
-        out_shape=[field_shape, pltpu.VMEM((blocks, 2 * rows, lanes), BF16)],
-        in_specs=[SM] + [VM] * 4,
-        out_specs=[VM] * 2,
-        compiler_params=params(32),
-        cost_estimate=cost(1 << 20, 4 << 20),
-        name="middle",
-    )(omega, edge_mass, near(direction), near(base), matrix)
+    rest, own = [
+        near(out)
+        for out in pl.pallas_call(
+            lambda *refs: middle(C4, *refs),
+            out_shape=[field_shape, own_shape],
+            in_specs=[SM] + [VM] * 4,
+            out_specs=[VM] * 2,
+            compiler_params=params(32),
+            cost_estimate=cost(1 << 20, 4 << 20),
+            name="middle",
+        )(omega, edge_mass, near(direction), near(base), matrix)
+    ]
     scale = 1.0 / math.sqrt(24.0 * count * lax.axis_size("freq"))
     efield, lfield, grad = pl.pallas_call(
         lambda *refs: second(scale, *refs),
@@ -274,7 +294,7 @@
         scratch_shapes=[ext, pltpu.VMEM((blocks, lanes), F32)],
         compiler_params=params(32),
         name="second",
-    )(links_t, omega, near(own), near(rest), matrix, *got, cell_edges)
+    )(links_t, omega, own, rest, matrix, *got, cell_edges)
     efield, lfield = pl.pallas_call(
         store,
         out_shape=[pltpu.HBM(flat, F32)] * 2,

time: 41.8 us -> 41.7 us (level)
  starting transfers between devices: 21.6 us -> 21.1 us
    pallas_call x2, Pallas kernels: 3.19 us -> 3.75 us  [the longest x1 2.79 us: local(): pl.pallas_call(split, out_shape=[matrix_shape, field_shape, own_shape], i...]
    ppermute x12, starting transfers between devices: 21.6 us -> 21.1 us  [swapped(): return lax.ppermute(value, axis, pairs)]
  transfers between devices with their start and end apart: 12 -> 12, of which waited for: 9 -> 8; matrix products, arithmetic and copies ran while one was open for 0% -> 0% of each run, Pallas kernels for 9% -> 11%
where the time goes in v4:
time: 41.7 us
  starting transfers between devices  21.1 us (51%)
  Pallas kernels  9.85 us (24%)
  waiting for transfers between devices  9.35 us (22%)
  between operations  0.76 us (2%)
  other arithmetic  0.61 us (1%)
    ppermute x12, starting transfers between devices, swapped(): return lax.ppermute(value, axis, pairs)  21.1 us
    ppermute x12, waiting for transfers between devices, swapped(): return lax.ppermute(value, axis, pairs)  9.35 us
    pallas_call x1, Pallas kernels, local(): pl.pallas_call(split, out_shape=[matrix_shape, field_shape, own_shape], i...  2.79 us
    pallas_call x1, Pallas kernels, local(): pl.pallas_call(lambda *refs: second(scale, *refs), out_shape=[flat_shape,...  2.12 us
    pallas_call x1, Pallas kernels, local(): pl.pallas_call(first, out_shape=[field_shape] * 2 + [tile_shape] * rounds...  1.92 us
    pallas_call x1, Pallas kernels, local(): pl.pallas_call(prepare, out_shape=[field_shape] + [tile_shape] * rounds,...  1.34 us
    pallas_call x1, Pallas kernels, local(): pl.pallas_call(lambda *refs: middle(C4, *refs), out_shape=[field_shape, o...  0.97 us
  transfers between devices with their start and end apart: 12, of which 8 were waited for; matrix products, arithmetic and copies ran while one was open for 0% of the time, Pallas kernels for 11%

profile of v4, /device:TPU:4, one launch (start us, length us, event | category | flops | bytes accessed | tf_op | source)
XLA Modules:
  0.0 41.7 jit_solution(14169355226219269581)
XLA Ops:
  0.7 1.3 %prepare.1 = (f32[32,16,128]{2,1,0:T(8,128)S(1)}, f32[16,16,128]{2,1,0:T(8,128)S(1)}, f32[16,16,128]{2,1,0:T(8,128)S(1)}, f32[16,16,128]{2,1,0:T(8,128)S(1)}, f32[16,16,128]{2,1,0:T(8,128)S(1)}) custom-call(s32[4,16]{1,0:T(4,128)} %tiles_ref.1, f32[256,128]{1,0:T(8,128)} %bitcast.9, f32[256,128]{1,0:T(8,128)} %bitcast.10), custom_call_target="tpu_custom_call" | custom-call | flops 3221225472 | bytes 1048576 | tf_op jit(solution)/shard_map/prepare/pallas_call | solution.py:233
  2.0 3.4 %collective-permute-start = (f32[16,16,128]{2,1,0:T(8,128)S(1)}, f32[16,16,128]{2,1,0:T(8,128)S(1)}, u32[]{:S(2)}, u32[]{:S(2)}) collective-permute-start(f32[16,16,128]{2,1,0:T(8,128)S(1)} %get-tuple-element.28), channel_id=1, source_target_pairs={{0,4},{1,5},{2,6},{3,7},{4,0},{5,1},{6,2},{7,3},{8,12},{9,13},{10,... | collective-permute-start | bytes 393224 | tf_op jit(solution)/shard_map/ppermute | solution.py:31
  5.4 1.9 %collective-permute-start.1 = (f32[16,16,128]{2,1,0:T(8,128)S(1)}, f32[16,16,128]{2,1,0:T(8,128)S(1)}, u32[]{:S(2)}, u32[]{:S(2)}) collective-permute-start(f32[16,16,128]{2,1,0:T(8,128)S(1)} %get-tuple-element.29), channel_id=1, source_target_pairs={{0,2},{1,3},{2,0},{3,1},{4,6},{5,7},{6,4},{7,5},{8,10},{9,11},{10,... | collective-permute-start | bytes 393224 | tf_op jit(solution)/shard_map/ppermute | solution.py:31
  7.3 1.2 %collective-permute-start.2 = (f32[16,16,128]{2,1,0:T(8,128)S(1)}, f32[16,16,128]{2,1,0:T(8,128)S(1)}, u32[]{:S(2)}, u32[]{:S(2)}) collective-permute-start(f32[16,16,128]{2,1,0:T(8,128)S(1)} %get-tuple-element.30), channel_id=1, source_target_pairs={{0,8},{1,9},{2,10},{3,11},{4,12},{5,13},{6,14},{7,15},{8,0},{9,1},... | collective-permute-start | bytes 393224 | tf_op jit(solution)/shard_map/ppermute | solution.py:31
  8.5 2.8 %split.1 = (bf16[32,512,256]{2,1,0:T(8,128)(2,1)S(1)}, f32[32,16,128]{2,1,0:T(8,128)S(1)}, bf16[32,32,128]{2,1,0:T(8,128)(2,1)S(1)}) custom-call(f32[2]{0:T(128)S(1)} %copy-done.4, f32[32,128]{1,0:T(8,128)S(1)} %copy-done.2, f32[32,16,128]{2,1,0:T(8,128)S(1)} %get-tuple-element.24.field_ref, f32[32,4,128,128]{3,2,1,0:T(8,128)S(1)} %copy-done), custom_call_target="tpu_custom_call" | custom-call | flops 8388608 | bytes 16777216 | tf_op jit(solution)/shard_map/split/pallas_call | solution.py:252
  11.3 0.5 %collective-permute-done.got1 = f32[16,16,128]{2,1,0:T(8,128)S(1)} collective-permute-done((f32[16,16,128]{2,1,0:T(8,128)S(1)}, f32[16,16,128]{2,1,0:T(8,128)S(1)}, u32[]{:S(2)}, u32[]{:S(2)}) %collective-permute-start) | collective-permute-done | bytes 131104 | tf_op jit(solution)/shard_map/ppermute | solution.py:31
  11.8 0.1 collective-permute-done.1.got2
  11.9 0.4 collective-permute-done.2.got3
  12.3 1.9 %first.1 = (f32[32,16,128]{2,1,0:T(8,128)S(1)}, f32[32,16,128]{2,1,0:T(8,128)S(1)}, f32[16,16,128]{2,1,0:T(8,128)S(1)}, f32[16,16,128]{2,1,0:T(8,128)S(1)}, f32[...) custom-call(s32[4,32]{1,0:T(4,128)S(1)} %bitcast.7, s32[4,16]{1,0:T(4,128)S(1)} %copy-done.5, ...), custom_call_target="tpu_custom_call" | custom-call | tf_op jit(solution)/shard_map/first/pallas_call | solution.py:262
  14.2 1.5 %collective-permute-start.4 = (f32[16,16,128]{2,1,0:T(8,128)S(1)}, f32[16,16,128]{2,1,0:T(8,128)S(1)}, u32[]{:S(2)}, u32[]{:S(2)}) collective-permute-start(f32[16,16,128]{2,1,0:T(8,128)S(1)} %get-tuple-element.36), channel_id=1, source_target_pairs={{0,4},{1,5},{2,6},{3,7},{4,0},{5,1},{6,2},{7,3},{8,12},{9,13},{10,... | collective-permute-start | bytes 393224 | tf_op jit(solution)/shard_map/ppermute | solution.py:31
  15.7 2.2 %collective-permute-start.5 = (f32[16,16,128]{2,1,0:T(8,128)S(1)}, f32[16,16,128]{2,1,0:T(8,128)S(1)}, u32[]{:S(2)}, u32[]{:S(2)}) collective-permute-start(f32[16,16,128]{2,1,0:T(8,128)S(1)} %get-tuple-element.37), channel_id=1, source_target_pairs={{0,2},{1,3},{2,0},{3,1},{4,6},{5,7},{6,4},{7,5},{8,10},{9,11},{10,... | collective-permute-start | bytes 393224 | tf_op jit(solution)/shard_map/ppermute | solution.py:31
  17.9 1.2 %collective-permute-start.6 = (f32[16,16,128]{2,1,0:T(8,128)S(1)}, f32[16,16,128]{2,1,0:T(8,128)S(1)}, u32[]{:S(2)}, u32[]{:S(2)}) collective-permute-start(f32[16,16,128]{2,1,0:T(8,128)S(1)} %get-tuple-element.38), channel_id=1, source_target_pairs={{0,8},{1,9},{2,10},{3,11},{4,12},{5,13},{6,14},{7,15},{8,0},{9,1},... | collective-permute-start | bytes 393224 | tf_op jit(solution)/shard_map/ppermute | solution.py:31
  19.1 1.0 %middle.1 = (f32[32,16,128]{2,1,0:T(8,128)S(1)}, bf16[32,32,128]{2,1,0:T(8,128)(2,1)S(1)}) custom-call(f32[2]{0:T(128)S(1)} %copy-done.4, f32[32,128]{1,0:T(8,128)S(1)} %copy-done.2, f32[32,16,128]{2,1,0:T(8,128)S(1)} %get-tuple-element.32.refs_2_, f32[32,16,128]{2,1,0:T(8,128)S(1)} %get-tuple-element.33.refs_3_, ...), custom_call_target="tpu_custom_call" | custom-call | flops 1048576 | bytes 4194304 | tf_op jit(solution)/shard_map/middle/pallas_call | solution.py:274
  20.0 3.1 %collective-permute-done.4.refs_5_ = f32[16,16,128]{2,1,0:T(8,128)S(1)} collective-permute-done((f32[16,16,128]{2,1,0:T(8,128)S(1)}, f32[16,16,128]{2,1,0:T(8,128)S(1)}, u32[]{:S(2)}, u32[]{:S(2)}) %collective-permute-start.4) | collective-permute-done | bytes 131104 | tf_op jit(solution)/shard_map/ppermute | solution.py:31
  23.1 0.1 collective-permute-done.5.refs_6_
  23.2 2.1 %second.1 = (f32[256,128]{1,0:T(8,128)S(1)}, f32[256,128]{1,0:T(8,128)S(1)}, f32[8,128]{1,0:T(8,128)S(1)}) custom-call(s32[4,32]{1,0:T(4,128)S(1)} %bitcast.8, f32[2]{0:T(128)S(1)} %copy-done.4, bf16[32,32,128]{2,1,0:T(8,128)(2,1)S(1)} %get-tuple-element.34.refs_2_, f32[32,16,128]{2,1,0:T(8,128)S(1)} %get-tuple-element.35.refs_3_, ...), custom_call_target="tpu_custom_call" | custom-call | tf_op jit(solution)/shard_map/second/pallas_call | solution.py:285
  25.3 3.3 %collective-permute-start.10 = (f32[8,128]{1,0:T(8,128)S(1)}, f32[8,128]{1,0:T(8,128)S(1)}, u32[]{:S(2)}, u32[]{:S(2)}) collective-permute-start(f32[8,128]{1,0:T(8,128)S(1)} %get-tuple-element.44), channel_id=1, source_target_pairs={{0,128},{32,160},{64,192},{96,224},{128,0},{160,32},{192,64},{224,... | collective-permute-start | bytes 12296 | tf_op jit(solution)/shard_map/ppermute | solution.py:31
  28.6 1.0 %collective-permute-start.9 = (f32[8,128]{1,0:T(8,128)S(1)}, f32[8,128]{1,0:T(8,128)S(1)}, u32[]{:S(2)}, u32[]{:S(2)}) collective-permute-start(f32[8,128]{1,0:T(8,128)S(1)} %get-tuple-element.44), channel_id=1, source_target_pairs={{0,192},{32,224},{64,128},{96,160},{128,64},{160,96},{192,0},{224,... | collective-permute-start | bytes 12296 | tf_op jit(solution)/shard_map/ppermute | solution.py:31
  29.7 0.9 %collective-permute-done.10 = f32[8,128]{1,0:T(8,128)S(1)} collective-permute-done((f32[8,128]{1,0:T(8,128)S(1)}, f32[8,128]{1,0:T(8,128)S(1)}, u32[]{:S(2)}, u32[]{:S(2)}) %collective-permute-start.10) | collective-permute-done | bytes 4128 | tf_op jit(solution)/shard_map/ppermute | solution.py:31
  30.5 2.9 %collective-permute-done.9 = f32[8,128]{1,0:T(8,128)S(1)} collective-permute-done((f32[8,128]{1,0:T(8,128)S(1)}, f32[8,128]{1,0:T(8,128)S(1)}, u32[]{:S(2)}, u32[]{:S(2)}) %collective-permute-start.9) | collective-permute-done | bytes 4128 | tf_op jit(solution)/shard_map/ppermute | solution.py:31
  33.4 5.4 %collective-permute-start.11 = (f32[8,128]{1,0:T(8,128)S(1)}, f32[8,128]{1,0:T(8,128)S(1)}, u32[]{:S(2)}, u32[]{:S(2)}) collective-permute-start(f32[8,128]{1,0:T(8,128)S(1)} %add_add_fusion), channel_id=1, source_target_pairs={{0,32},{32,0},{64,96},{96,64},{128,160},{160,128},{192,224},{224,1... | collective-permute-start | bytes 12296 | tf_op jit(solution)/shard_map/ppermute | solution.py:31
  38.9 0.7 %store.1 = (f32[256,128]{1,0:T(8,128)}, f32[256,128]{1,0:T(8,128)}) custom-call(f32[256,128]{1,0:T(8,128)S(1)} %get-tuple-element.40.fwd_ref, f32[256,128]{1,0:T(8,128)S(1)} %get-tuple-element.41.adj_ref), custom_call_target="tpu_custom_call" | custom-call | flops 1024 | bytes 1048576 | tf_op jit(solution)/shard_map/store/pallas_call | solution.py:298
  39.6 1.5 %collective-permute-done.11 = f32[8,128]{1,0:T(8,128)S(1)} collective-permute-done((f32[8,128]{1,0:T(8,128)S(1)}, f32[8,128]{1,0:T(8,128)S(1)}, u32[]{:S(2)}, u32[]{:S(2)}) %collective-permute-start.11) | collective-permute-done | bytes 4128 | tf_op jit(solution)/shard_map/ppermute | solution.py:31
  41.0 0.6 %bitcast_subtract_fusion = f32[1024]{0:T(1024)} fusion(f32[1024]{0:T(1024)S(1)} %copy-done.6, f32[8,128]{1,0:T(8,128)S(1)} %add_add_fusion, f32[8,128]{1,0:T(8,128)S(1)} %collective-permute-done.11), kind=kLoop, calls=%fused_computation | loop fusion | flops 6144 | bytes 16384 | tf_op jit(solution)/shard_map/sub | solution.py:312
  (22 shorter events, 0.1 us)
Async XLA Ops:
  0.6 7.9 %copy-start.4 = (f32[2]{0:T(128)S(1)}, f32[2]{0:T(128)}, u32[]{:S(2)}) copy-start(f32[2]{0:T(128)} %refs_1_.3) | copy-start | bytes 28
  0.6 7.9 %copy-start.2 = (f32[32,128]{1,0:T(8,128)S(1)}, f32[32,128]{1,0:T(8,128)}, u32[]{:S(2)}) copy-start(f32[32,128]{1,0:T(8,128)} %refs_1_.2) | copy-start | bytes 49156
  0.7 7.9 %copy-start = (f32[32,4,128,128]{3,2,1,0:T(8,128)S(1)}, f32[32,4,128,128]{3,2,1,0:T(8,128)}, u32[]{:S(2)}) copy-start(f32[32,4,128,128]{3,2,1,0:T(8,128)} %curl_ref.1) | copy-start | bytes 25165828
  0.7 11.6 %copy-start.3 = (s32[32,4]{0,1:T(4,128)S(1)}, s32[32,4]{0,1:T(4,128)}, u32[]{:S(2)}) copy-start(s32[32,4]{0,1:T(4,128)} %param.12) | copy-start | bytes 1540
  0.7 11.6 %copy-start.5 = (s32[4,16]{1,0:T(4,128)S(1)}, s32[4,16]{1,0:T(4,128)}, u32[]{:S(2)}) copy-start(s32[4,16]{1,0:T(4,128)} %tiles_ref.1) | copy-start | bytes 772
  2.0 9.8 %collective-permute-start = (f32[16,16,128]{2,1,0:T(8,128)S(1)}, f32[16,16,128]{2,1,0:T(8,128)S(1)}, u32[]{:S(2)}, u32[]{:S(2)}) collective-permute-start(f32[16,16,128]{2,1,0:T(8,128)S(1)} %get-tuple-element.28), channel_id=1, source_target_pairs={{0,4},{1,5},{2,6},{3,7},{4,0},{5,1},{6,2},{7,3},{8,12},{9,13},{10,... | collective-permute-start | bytes 393224 | tf_op jit(solution)/shard_map/ppermute | solution.py:31
  5.4 6.5 %collective-permute-start.1 = (f32[16,16,128]{2,1,0:T(8,128)S(1)}, f32[16,16,128]{2,1,0:T(8,128)S(1)}, u32[]{:S(2)}, u32[]{:S(2)}) collective-permute-start(f32[16,16,128]{2,1,0:T(8,128)S(1)} %get-tuple-element.29), channel_id=1, source_target_pairs={{0,2},{1,3},{2,0},{3,1},{4,6},{5,7},{6,4},{7,5},{8,10},{9,11},{10,... | collective-permute-start | bytes 393224 | tf_op jit(solution)/shard_map/ppermute | solution.py:31
  7.3 5.0 %collective-permute-start.2 = (f32[16,16,128]{2,1,0:T(8,128)S(1)}, f32[16,16,128]{2,1,0:T(8,128)S(1)}, u32[]{:S(2)}, u32[]{:S(2)}) collective-permute-start(f32[16,16,128]{2,1,0:T(8,128)S(1)} %get-tuple-element.30), channel_id=1, source_target_pairs={{0,8},{1,9},{2,10},{3,11},{4,12},{5,13},{6,14},{7,15},{8,0},{9,1},... | collective-permute-start | bytes 393224 | tf_op jit(solution)/shard_map/ppermute | solution.py:31
  8.5 3.8 %collective-permute-start.3 = (f32[16,16,128]{2,1,0:T(8,128)S(1)}, f32[16,16,128]{2,1,0:T(8,128)S(1)}, u32[]{:S(2)}, u32[]{:S(2)}) collective-permute-start(f32[16,16,128]{2,1,0:T(8,128)S(1)} %get-tuple-element.31), channel_id=1, source_target_pairs={{0,1},{1,0},{2,3},{3,2},{4,5},{5,4},{6,7},{7,6},{8,9},{9,8},{10,11... | collective-permute-start | bytes 393224 | tf_op jit(solution)/shard_map/ppermute | solution.py:31
  12.3 10.9 %copy-start.1 = (s32[12,1024]{1,0:T(8,128)S(1)}, s32[12,1024]{1,0:T(8,128)}, u32[]{:S(2)}) copy-start(s32[12,1024]{1,0:T(8,128)} %refs_9_.1) | copy-start | bytes 147460
  14.2 8.9 %collective-permute-start.4 = (f32[16,16,128]{2,1,0:T(8,128)S(1)}, f32[16,16,128]{2,1,0:T(8,128)S(1)}, u32[]{:S(2)}, u32[]{:S(2)}) collective-permute-start(f32[16,16,128]{2,1,0:T(8,128)S(1)} %get-tuple-element.36), channel_id=1, source_target_pairs={{0,4},{1,5},{2,6},{3,7},{4,0},{5,1},{6,2},{7,3},{8,12},{9,13},{10,... | collective-permute-start | bytes 393224 | tf_op jit(solution)/shard_map/ppermute | solution.py:31
  15.7 7.5 %collective-permute-start.5 = (f32[16,16,128]{2,1,0:T(8,128)S(1)}, f32[16,16,128]{2,1,0:T(8,128)S(1)}, u32[]{:S(2)}, u32[]{:S(2)}) collective-permute-start(f32[16,16,128]{2,1,0:T(8,128)S(1)} %get-tuple-element.37), channel_id=1, source_target_pairs={{0,2},{1,3},{2,0},{3,1},{4,6},{5,7},{6,4},{7,5},{8,10},{9,11},{10,... | collective-permute-start | bytes 393224 | tf_op jit(solution)/shard_map/ppermute | solution.py:31
  17.9 5.3 %collective-permute-start.6 = (f32[16,16,128]{2,1,0:T(8,128)S(1)}, f32[16,16,128]{2,1,0:T(8,128)S(1)}, u32[]{:S(2)}, u32[]{:S(2)}) collective-permute-start(f32[16,16,128]{2,1,0:T(8,128)S(1)} %get-tuple-element.38), channel_id=1, source_target_pairs={{0,8},{1,9},{2,10},{3,11},{4,12},{5,13},{6,14},{7,15},{8,0},{9,1},... | collective-permute-start | bytes 393224 | tf_op jit(solution)/shard_map/ppermute | solution.py:31
  19.1 4.1 %collective-permute-start.7 = (f32[16,16,128]{2,1,0:T(8,128)S(1)}, f32[16,16,128]{2,1,0:T(8,128)S(1)}, u32[]{:S(2)}, u32[]{:S(2)}) collective-permute-start(f32[16,16,128]{2,1,0:T(8,128)S(1)} %get-tuple-element.39), channel_id=1, source_target_pairs={{0,1},{1,0},{2,3},{3,2},{4,5},{5,4},{6,7},{7,6},{8,9},{9,8},{10,11... | collective-permute-start | bytes 393224 | tf_op jit(solution)/shard_map/ppermute | solution.py:31
  19.1 22.0 %copy-start.6 = (f32[1024]{0:T(1024)S(1)}, f32[1024]{0:T(1024)}, u32[]{:S(2)}) copy-start(f32[1024]{0:T(1024)} %param.17) | copy-start | bytes 12292
  25.3 5.2 %collective-permute-start.10 = (f32[8,128]{1,0:T(8,128)S(1)}, f32[8,128]{1,0:T(8,128)S(1)}, u32[]{:S(2)}, u32[]{:S(2)}) collective-permute-start(f32[8,128]{1,0:T(8,128)S(1)} %get-tuple-element.44), channel_id=1, source_target_pairs={{0,128},{32,160},{64,192},{96,224},{128,0},{160,32},{192,64},{224,... | collective-permute-start | bytes 12296 | tf_op jit(solution)/shard_map/ppermute | solution.py:31
  28.6 4.8 %collective-permute-start.9 = (f32[8,128]{1,0:T(8,128)S(1)}, f32[8,128]{1,0:T(8,128)S(1)}, u32[]{:S(2)}, u32[]{:S(2)}) collective-permute-start(f32[8,128]{1,0:T(8,128)S(1)} %get-tuple-element.44), channel_id=1, source_target_pairs={{0,192},{32,224},{64,128},{96,160},{128,64},{160,96},{192,0},{224,... | collective-permute-start | bytes 12296 | tf_op jit(solution)/shard_map/ppermute | solution.py:31
  29.7 3.8 %collective-permute-start.8 = (f32[8,128]{1,0:T(8,128)S(1)}, f32[8,128]{1,0:T(8,128)S(1)}, u32[]{:S(2)}, u32[]{:S(2)}) collective-permute-start(f32[8,128]{1,0:T(8,128)S(1)} %get-tuple-element.44), channel_id=1, source_target_pairs={{0,64},{32,96},{64,0},{96,32},{128,192},{160,224},{192,128},{224,1... | collective-permute-start | bytes 12296 | tf_op jit(solution)/shard_map/ppermute | solution.py:31
  33.4 7.6 %collective-permute-start.11 = (f32[8,128]{1,0:T(8,128)S(1)}, f32[8,128]{1,0:T(8,128)S(1)}, u32[]{:S(2)}, u32[]{:S(2)}) collective-permute-start(f32[8,128]{1,0:T(8,128)S(1)} %add_add_fusion), channel_id=1, source_target_pairs={{0,32},{32,0},{64,96},{96,64},{128,160},{160,128},{192,224},{224,1... | collective-permute-start | bytes 12296 | tf_op jit(solution)/shard_map/ppermute | solution.py:31

commit v5 on v4

--- a/solution.py
+++ b/solution.py
@@ -169,7 +169,7 @@
 
 def second(
     scale, links_ref, omega_ref, own_ref, rest_ref, matrix_ref, got1, got2, got3, got4,
-    cells_ref, fwd_ref, adj_ref, grad_ref, ext, table,
+    cells_ref, field_ref, grad_ref, ext, table,
 ):
     blocks, rows, lanes = rest_ref.shape
     half = rows // 2
@@ -178,10 +178,8 @@
     omega, _ = frequency_rows(omega_ref, rows, lanes)
     for b in range(blocks):
         x = rest_ref[b] - C4 * curl_row(b, links_ref, matrix_ref, ext, 1)
-        efield, lfield = x[:half], x[half:]
-        fwd_ref[pl.ds(b, half, stride=blocks), :] = efield
-        adj_ref[pl.ds(b, half, stride=blocks), :] = lfield
-        prod = omega[:half] * efield * other(lfield)
+        field_ref[b] = x
+        prod = omega[:half] * x[:half] * other(x[half:])
         table[b : b + 1] = jnp.sum(prod, axis=0, keepdims=True)
     edges, cells = cells_ref.shape
 
@@ -205,11 +203,15 @@
         grad_ref[c + 1 : c + 2] = (total(find(right[:8])) + total(last[edges - 8 :])) * scale
 
 
-def store(fwd_ref, adj_ref, fwd_hbm, adj_hbm, sems):
+def store(field_ref, fwd_hbm, adj_hbm, fwd_ref, adj_ref, sems):
+    blocks, rows, _ = field_ref.shape
+    half = rows // 2
     pairs = ((fwd_ref, fwd_hbm), (adj_ref, adj_hbm))
     copies = [pltpu.make_async_copy(a, b, sems.at[i]) for i, (a, b) in enumerate(pairs)]
-    for copy in copies:
-        copy.start()
+    for s in range(2):
+        for b in range(blocks):
+            pairs[s][0][pl.ds(b, half, stride=blocks), :] = field_ref[b, s * half : (s + 1) * half]
+        copies[s].start()
     for copy in copies:
         copy.wait()
 
@@ -282,15 +284,14 @@
         )(omega, edge_mass, near(direction), near(base), matrix)
     ]
     scale = 1.0 / math.sqrt(24.0 * count * lax.axis_size("freq"))
-    efield, lfield, grad = pl.pallas_call(
+    fields, grad = pl.pallas_call(
         lambda *refs: second(scale, *refs),
         out_shape=[
-            flat_shape,
-            flat_shape,
+            field_shape,
             pltpu.VMEM((log_cond.shape[0] // lanes, lanes), F32),
         ],
         in_specs=[SM] * 2 + [VM] * (4 + rounds),
-        out_specs=[VM] * 3,
+        out_specs=[VM] * 2,
         scratch_shapes=[ext, pltpu.VMEM((blocks, lanes), F32)],
         compiler_params=params(32),
         name="second",
@@ -298,13 +299,13 @@
     efield, lfield = pl.pallas_call(
         store,
         out_shape=[pltpu.HBM(flat, F32)] * 2,
-        in_specs=[VM] * 2,
+        in_specs=[VM],
         out_specs=[HB] * 2,
-        scratch_shapes=[DMA((2,))],
+        scratch_shapes=[flat_shape, flat_shape, DMA((2,))],
         compiler_params=params(8),
         cost_estimate=cost(1 << 10, 1 << 20),
         name="store",
-    )(near(efield), near(lfield))
+    )(near(fields))
     got = [swapped(grad, "freq", mask) for mask in (2, 6, 4)]
     grad = grad + got[0] + got[1] + got[2]
     grad = grad + swapped(grad, "freq", 1)

time: 41.7 us -> 41.7 us (level)
  no operation moved by 1% of the time
where the time goes in v5:
time: 41.7 us; the launch traced here: 41.6 us
  starting transfers between devices  21.1 us (51%)
  Pallas kernels  9.88 us (24%)
  waiting for transfers between devices  9.22 us (22%)
  between operations  0.76 us (2%)
  other arithmetic  0.61 us (1%)
    ppermute x12, starting transfers between devices, swapped(): return lax.ppermute(value, axis, pairs)  21.1 us
    ppermute x12, waiting for transfers between devices, swapped(): return lax.ppermute(value, axis, pairs)  9.22 us
    pallas_call x1, Pallas kernels, local(): pl.pallas_call(split, out_shape=[matrix_shape, field_shape, own_shape], i...  2.79 us
    pallas_call x1, Pallas kernels, local(): pl.pallas_call(lambda *refs: second(scale, *refs), out_shape=[field_shape...  2.04 us
    pallas_call x1, Pallas kernels, local(): pl.pallas_call(first, out_shape=[field_shape] * 2 + [tile_shape] * rounds...  1.92 us
    pallas_call x1, Pallas kernels, local(): pl.pallas_call(prepare, out_shape=[field_shape] + [tile_shape] * rounds,...  1.34 us
    pallas_call x1, Pallas kernels, local(): pl.pallas_call(lambda *refs: middle(C4, *refs), out_shape=[field_shape, o...  0.97 us
  transfers between devices with their start and end apart: 12, of which 8 were waited for; matrix products, arithmetic and copies ran while one was open for 0% of the time, Pallas kernels for 11%

profile of v5, /device:TPU:4, one launch (start us, length us, event | category | flops | bytes accessed | tf_op | source)
XLA Modules:
  0.0 41.6 jit_solution(7403154599435125332)
XLA Ops:
  0.7 1.3 %prepare.1 = (f32[32,16,128]{2,1,0:T(8,128)S(1)}, f32[16,16,128]{2,1,0:T(8,128)S(1)}, f32[16,16,128]{2,1,0:T(8,128)S(1)}, f32[16,16,128]{2,1,0:T(8,128)S(1)}, f32[16,16,128]{2,1,0:T(8,128)S(1)}) custom-call(s32[4,16]{1,0:T(4,128)} %tiles_ref.1, f32[256,128]{1,0:T(8,128)} %bitcast.9, f32[256,128]{1,0:T(8,128)} %bitcast.10), custom_call_target="tpu_custom_call" | custom-call | flops 3221225472 | bytes 1048576 | tf_op jit(solution)/shard_map/prepare/pallas_call | solution.py:235
  2.0 3.4 %collective-permute-start = (f32[16,16,128]{2,1,0:T(8,128)S(1)}, f32[16,16,128]{2,1,0:T(8,128)S(1)}, u32[]{:S(2)}, u32[]{:S(2)}) collective-permute-start(f32[16,16,128]{2,1,0:T(8,128)S(1)} %get-tuple-element.27), channel_id=1, source_target_pairs={{0,4},{1,5},{2,6},{3,7},{4,0},{5,1},{6,2},{7,3},{8,12},{9,13},{10,... | collective-permute-start | bytes 393224 | tf_op jit(solution)/shard_map/ppermute | solution.py:31
  5.4 1.9 %collective-permute-start.1 = (f32[16,16,128]{2,1,0:T(8,128)S(1)}, f32[16,16,128]{2,1,0:T(8,128)S(1)}, u32[]{:S(2)}, u32[]{:S(2)}) collective-permute-start(f32[16,16,128]{2,1,0:T(8,128)S(1)} %get-tuple-element.28), channel_id=1, source_target_pairs={{0,2},{1,3},{2,0},{3,1},{4,6},{5,7},{6,4},{7,5},{8,10},{9,11},{10,... | collective-permute-start | bytes 393224 | tf_op jit(solution)/shard_map/ppermute | solution.py:31
  7.3 1.2 %collective-permute-start.2 = (f32[16,16,128]{2,1,0:T(8,128)S(1)}, f32[16,16,128]{2,1,0:T(8,128)S(1)}, u32[]{:S(2)}, u32[]{:S(2)}) collective-permute-start(f32[16,16,128]{2,1,0:T(8,128)S(1)} %get-tuple-element.29), channel_id=1, source_target_pairs={{0,8},{1,9},{2,10},{3,11},{4,12},{5,13},{6,14},{7,15},{8,0},{9,1},... | collective-permute-start | bytes 393224 | tf_op jit(solution)/shard_map/ppermute | solution.py:31
  8.5 2.8 %split.1 = (bf16[32,512,256]{2,1,0:T(8,128)(2,1)S(1)}, f32[32,16,128]{2,1,0:T(8,128)S(1)}, bf16[32,32,128]{2,1,0:T(8,128)(2,1)S(1)}) custom-call(f32[2]{0:T(128)S(1)} %copy-done.4, f32[32,128]{1,0:T(8,128)S(1)} %copy-done.2, f32[32,16,128]{2,1,0:T(8,128)S(1)} %get-tuple-element.23.field_ref, f32[32,4,128,128]{3,2,1,0:T(8,128)S(1)} %copy-done), custom_call_target="tpu_custom_call" | custom-call | flops 8388608 | bytes 16777216 | tf_op jit(solution)/shard_map/split/pallas_call | solution.py:254
  11.3 0.5 %collective-permute-done.got1 = f32[16,16,128]{2,1,0:T(8,128)S(1)} collective-permute-done((f32[16,16,128]{2,1,0:T(8,128)S(1)}, f32[16,16,128]{2,1,0:T(8,128)S(1)}, u32[]{:S(2)}, u32[]{:S(2)}) %collective-permute-start) | collective-permute-done | bytes 131104 | tf_op jit(solution)/shard_map/ppermute | solution.py:31
  11.8 0.1 collective-permute-done.1.got2
  11.9 0.4 collective-permute-done.2.got3
  12.3 1.9 %first.1 = (f32[32,16,128]{2,1,0:T(8,128)S(1)}, f32[32,16,128]{2,1,0:T(8,128)S(1)}, f32[16,16,128]{2,1,0:T(8,128)S(1)}, f32[16,16,128]{2,1,0:T(8,128)S(1)}, f32[...) custom-call(s32[4,32]{1,0:T(4,128)S(1)} %bitcast.7, s32[4,16]{1,0:T(4,128)S(1)} %copy-done.5, ...), custom_call_target="tpu_custom_call" | custom-call | tf_op jit(solution)/shard_map/first/pallas_call | solution.py:264
  14.2 1.5 %collective-permute-start.4 = (f32[16,16,128]{2,1,0:T(8,128)S(1)}, f32[16,16,128]{2,1,0:T(8,128)S(1)}, u32[]{:S(2)}, u32[]{:S(2)}) collective-permute-start(f32[16,16,128]{2,1,0:T(8,128)S(1)} %get-tuple-element.35), channel_id=1, source_target_pairs={{0,4},{1,5},{2,6},{3,7},{4,0},{5,1},{6,2},{7,3},{8,12},{9,13},{10,... | collective-permute-start | bytes 393224 | tf_op jit(solution)/shard_map/ppermute | solution.py:31
  15.7 2.1 %collective-permute-start.5 = (f32[16,16,128]{2,1,0:T(8,128)S(1)}, f32[16,16,128]{2,1,0:T(8,128)S(1)}, u32[]{:S(2)}, u32[]{:S(2)}) collective-permute-start(f32[16,16,128]{2,1,0:T(8,128)S(1)} %get-tuple-element.36), channel_id=1, source_target_pairs={{0,2},{1,3},{2,0},{3,1},{4,6},{5,7},{6,4},{7,5},{8,10},{9,11},{10,... | collective-permute-start | bytes 393224 | tf_op jit(solution)/shard_map/ppermute | solution.py:31
  17.9 1.2 %collective-permute-start.6 = (f32[16,16,128]{2,1,0:T(8,128)S(1)}, f32[16,16,128]{2,1,0:T(8,128)S(1)}, u32[]{:S(2)}, u32[]{:S(2)}) collective-permute-start(f32[16,16,128]{2,1,0:T(8,128)S(1)} %get-tuple-element.37), channel_id=1, source_target_pairs={{0,8},{1,9},{2,10},{3,11},{4,12},{5,13},{6,14},{7,15},{8,0},{9,1},... | collective-permute-start | bytes 393224 | tf_op jit(solution)/shard_map/ppermute | solution.py:31
  19.1 1.0 %middle.1 = (f32[32,16,128]{2,1,0:T(8,128)S(1)}, bf16[32,32,128]{2,1,0:T(8,128)(2,1)S(1)}) custom-call(f32[2]{0:T(128)S(1)} %copy-done.4, f32[32,128]{1,0:T(8,128)S(1)} %copy-done.2, f32[32,16,128]{2,1,0:T(8,128)S(1)} %get-tuple-element.31.refs_2_, f32[32,16,128]{2,1,0:T(8,128)S(1)} %get-tuple-element.32.refs_3_, ...), custom_call_target="tpu_custom_call" | custom-call | flops 1048576 | bytes 4194304 | tf_op jit(solution)/shard_map/middle/pallas_call | solution.py:276
  20.0 3.1 %collective-permute-done.4.refs_5_ = f32[16,16,128]{2,1,0:T(8,128)S(1)} collective-permute-done((f32[16,16,128]{2,1,0:T(8,128)S(1)}, f32[16,16,128]{2,1,0:T(8,128)S(1)}, u32[]{:S(2)}, u32[]{:S(2)}) %collective-permute-start.4) | collective-permute-done | bytes 131104 | tf_op jit(solution)/shard_map/ppermute | solution.py:31
  23.1 0.1 collective-permute-done.5.refs_6_
  23.2 2.0 %second.1 = (f32[32,16,128]{2,1,0:T(8,128)S(1)}, f32[8,128]{1,0:T(8,128)S(1)}) custom-call(s32[4,32]{1,0:T(4,128)S(1)} %bitcast.8, f32[2]{0:T(128)S(1)} %copy-done.4, bf16[32,32,128]{2,1,0:T(8,128)(2,1)S(1)} %get-tuple-element.33.refs_2_, f32[32,16,128]{2,1,0:T(8,128)S(1)} %get-tuple-element.34.refs_3_, ...), custom_call_target="tpu_custom_call" | custom-call | tf_op jit(solution)/shard_map/second/pallas_call | solution.py:287
  25.3 3.3 %collective-permute-start.10 = (f32[8,128]{1,0:T(8,128)S(1)}, f32[8,128]{1,0:T(8,128)S(1)}, u32[]{:S(2)}, u32[]{:S(2)}) collective-permute-start(f32[8,128]{1,0:T(8,128)S(1)} %get-tuple-element.42), channel_id=1, source_target_pairs={{0,128},{32,160},{64,192},{96,224},{128,0},{160,32},{192,64},{224,... | collective-permute-start | bytes 12296 | tf_op jit(solution)/shard_map/ppermute | solution.py:31
  28.5 1.1 %collective-permute-start.9 = (f32[8,128]{1,0:T(8,128)S(1)}, f32[8,128]{1,0:T(8,128)S(1)}, u32[]{:S(2)}, u32[]{:S(2)}) collective-permute-start(f32[8,128]{1,0:T(8,128)S(1)} %get-tuple-element.42), channel_id=1, source_target_pairs={{0,192},{32,224},{64,128},{96,160},{128,64},{160,96},{192,0},{224,... | collective-permute-start | bytes 12296 | tf_op jit(solution)/shard_map/ppermute | solution.py:31
  29.6 0.9 %collective-permute-done.10 = f32[8,128]{1,0:T(8,128)S(1)} collective-permute-done((f32[8,128]{1,0:T(8,128)S(1)}, f32[8,128]{1,0:T(8,128)S(1)}, u32[]{:S(2)}, u32[]{:S(2)}) %collective-permute-start.10) | collective-permute-done | bytes 4128 | tf_op jit(solution)/shard_map/ppermute | solution.py:31
  30.5 2.9 %collective-permute-done.9 = f32[8,128]{1,0:T(8,128)S(1)} collective-permute-done((f32[8,128]{1,0:T(8,128)S(1)}, f32[8,128]{1,0:T(8,128)S(1)}, u32[]{:S(2)}, u32[]{:S(2)}) %collective-permute-start.9) | collective-permute-done | bytes 4128 | tf_op jit(solution)/shard_map/ppermute | solution.py:31
  33.4 5.4 %collective-permute-start.11 = (f32[8,128]{1,0:T(8,128)S(1)}, f32[8,128]{1,0:T(8,128)S(1)}, u32[]{:S(2)}, u32[]{:S(2)}) collective-permute-start(f32[8,128]{1,0:T(8,128)S(1)} %add_add_fusion), channel_id=1, source_target_pairs={{0,32},{32,0},{64,96},{96,64},{128,160},{160,128},{192,224},{224,1... | collective-permute-start | bytes 12296 | tf_op jit(solution)/shard_map/ppermute | solution.py:31
  38.8 0.8 %store.1 = (f32[256,128]{1,0:T(8,128)}, f32[256,128]{1,0:T(8,128)}) custom-call(f32[32,16,128]{2,1,0:T(8,128)S(1)} %get-tuple-element.39.field_ref), custom_call_target="tpu_custom_call" | custom-call | flops 1024 | bytes 1048576 | tf_op jit(solution)/shard_map/store/pallas_call | solution.py:299
  39.6 1.3 %collective-permute-done.11 = f32[8,128]{1,0:T(8,128)S(1)} collective-permute-done((f32[8,128]{1,0:T(8,128)S(1)}, f32[8,128]{1,0:T(8,128)S(1)}, u32[]{:S(2)}, u32[]{:S(2)}) %collective-permute-start.11) | collective-permute-done | bytes 4128 | tf_op jit(solution)/shard_map/ppermute | solution.py:31
  41.0 0.6 %bitcast_subtract_fusion = f32[1024]{0:T(1024)} fusion(f32[1024]{0:T(1024)S(1)} %copy-done.6, f32[8,128]{1,0:T(8,128)S(1)} %add_add_fusion, f32[8,128]{1,0:T(8,128)S(1)} %collective-permute-done.11), kind=kLoop, calls=%fused_computation | loop fusion | flops 6144 | bytes 16384 | tf_op jit(solution)/shard_map/sub | solution.py:313
  (22 shorter events, 0.1 us)
Async XLA Ops:
  0.6 7.9 %copy-start.4 = (f32[2]{0:T(128)S(1)}, f32[2]{0:T(128)}, u32[]{:S(2)}) copy-start(f32[2]{0:T(128)} %refs_1_.3) | copy-start | bytes 28
  0.6 7.9 %copy-start.2 = (f32[32,128]{1,0:T(8,128)S(1)}, f32[32,128]{1,0:T(8,128)}, u32[]{:S(2)}) copy-start(f32[32,128]{1,0:T(8,128)} %refs_1_.2) | copy-start | bytes 49156
  0.7 7.9 %copy-start = (f32[32,4,128,128]{3,2,1,0:T(8,128)S(1)}, f32[32,4,128,128]{3,2,1,0:T(8,128)}, u32[]{:S(2)}) copy-start(f32[32,4,128,128]{3,2,1,0:T(8,128)} %curl_ref.1) | copy-start | bytes 25165828
  0.7 11.6 %copy-start.3 = (s32[32,4]{0,1:T(4,128)S(1)}, s32[32,4]{0,1:T(4,128)}, u32[]{:S(2)}) copy-start(s32[32,4]{0,1:T(4,128)} %param.12) | copy-start | bytes 1540
  0.7 11.6 %copy-start.5 = (s32[4,16]{1,0:T(4,128)S(1)}, s32[4,16]{1,0:T(4,128)}, u32[]{:S(2)}) copy-start(s32[4,16]{1,0:T(4,128)} %tiles_ref.1) | copy-start | bytes 772
  2.0 9.8 %collective-permute-start = (f32[16,16,128]{2,1,0:T(8,128)S(1)}, f32[16,16,128]{2,1,0:T(8,128)S(1)}, u32[]{:S(2)}, u32[]{:S(2)}) collective-permute-start(f32[16,16,128]{2,1,0:T(8,128)S(1)} %get-tuple-element.27), channel_id=1, source_target_pairs={{0,4},{1,5},{2,6},{3,7},{4,0},{5,1},{6,2},{7,3},{8,12},{9,13},{10,... | collective-permute-start | bytes 393224 | tf_op jit(solution)/shard_map/ppermute | solution.py:31
  5.4 6.5 %collective-permute-start.1 = (f32[16,16,128]{2,1,0:T(8,128)S(1)}, f32[16,16,128]{2,1,0:T(8,128)S(1)}, u32[]{:S(2)}, u32[]{:S(2)}) collective-permute-start(f32[16,16,128]{2,1,0:T(8,128)S(1)} %get-tuple-element.28), channel_id=1, source_target_pairs={{0,2},{1,3},{2,0},{3,1},{4,6},{5,7},{6,4},{7,5},{8,10},{9,11},{10,... | collective-permute-start | bytes 393224 | tf_op jit(solution)/shard_map/ppermute | solution.py:31
  7.3 5.0 %collective-permute-start.2 = (f32[16,16,128]{2,1,0:T(8,128)S(1)}, f32[16,16,128]{2,1,0:T(8,128)S(1)}, u32[]{:S(2)}, u32[]{:S(2)}) collective-permute-start(f32[16,16,128]{2,1,0:T(8,128)S(1)} %get-tuple-element.29), channel_id=1, source_target_pairs={{0,8},{1,9},{2,10},{3,11},{4,12},{5,13},{6,14},{7,15},{8,0},{9,1},... | collective-permute-start | bytes 393224 | tf_op jit(solution)/shard_map/ppermute | solution.py:31
  8.5 3.8 %collective-permute-start.3 = (f32[16,16,128]{2,1,0:T(8,128)S(1)}, f32[16,16,128]{2,1,0:T(8,128)S(1)}, u32[]{:S(2)}, u32[]{:S(2)}) collective-permute-start(f32[16,16,128]{2,1,0:T(8,128)S(1)} %get-tuple-element.30), channel_id=1, source_target_pairs={{0,1},{1,0},{2,3},{3,2},{4,5},{5,4},{6,7},{7,6},{8,9},{9,8},{10,11... | collective-permute-start | bytes 393224 | tf_op jit(solution)/shard_map/ppermute | solution.py:31
  12.3 10.9 %copy-start.1 = (s32[12,1024]{1,0:T(8,128)S(1)}, s32[12,1024]{1,0:T(8,128)}, u32[]{:S(2)}) copy-start(s32[12,1024]{1,0:T(8,128)} %refs_9_.1) | copy-start | bytes 147460
  14.2 8.9 %collective-permute-start.4 = (f32[16,16,128]{2,1,0:T(8,128)S(1)}, f32[16,16,128]{2,1,0:T(8,128)S(1)}, u32[]{:S(2)}, u32[]{:S(2)}) collective-permute-start(f32[16,16,128]{2,1,0:T(8,128)S(1)} %get-tuple-element.35), channel_id=1, source_target_pairs={{0,4},{1,5},{2,6},{3,7},{4,0},{5,1},{6,2},{7,3},{8,12},{9,13},{10,... | collective-permute-start | bytes 393224 | tf_op jit(solution)/shard_map/ppermute | solution.py:31
  15.7 7.5 %collective-permute-start.5 = (f32[16,16,128]{2,1,0:T(8,128)S(1)}, f32[16,16,128]{2,1,0:T(8,128)S(1)}, u32[]{:S(2)}, u32[]{:S(2)}) collective-permute-start(f32[16,16,128]{2,1,0:T(8,128)S(1)} %get-tuple-element.36), channel_id=1, source_target_pairs={{0,2},{1,3},{2,0},{3,1},{4,6},{5,7},{6,4},{7,5},{8,10},{9,11},{10,... | collective-permute-start | bytes 393224 | tf_op jit(solution)/shard_map/ppermute | solution.py:31
  17.9 5.3 %collective-permute-start.6 = (f32[16,16,128]{2,1,0:T(8,128)S(1)}, f32[16,16,128]{2,1,0:T(8,128)S(1)}, u32[]{:S(2)}, u32[]{:S(2)}) collective-permute-start(f32[16,16,128]{2,1,0:T(8,128)S(1)} %get-tuple-element.37), channel_id=1, source_target_pairs={{0,8},{1,9},{2,10},{3,11},{4,12},{5,13},{6,14},{7,15},{8,0},{9,1},... | collective-permute-start | bytes 393224 | tf_op jit(solution)/shard_map/ppermute | solution.py:31
  19.1 4.2 %collective-permute-start.7 = (f32[16,16,128]{2,1,0:T(8,128)S(1)}, f32[16,16,128]{2,1,0:T(8,128)S(1)}, u32[]{:S(2)}, u32[]{:S(2)}) collective-permute-start(f32[16,16,128]{2,1,0:T(8,128)S(1)} %get-tuple-element.38), channel_id=1, source_target_pairs={{0,1},{1,0},{2,3},{3,2},{4,5},{5,4},{6,7},{7,6},{8,9},{9,8},{10,11... | collective-permute-start | bytes 393224 | tf_op jit(solution)/shard_map/ppermute | solution.py:31
  19.1 21.9 %copy-start.6 = (f32[1024]{0:T(1024)S(1)}, f32[1024]{0:T(1024)}, u32[]{:S(2)}) copy-start(f32[1024]{0:T(1024)} %param.17) | copy-start | bytes 12292
  25.3 5.2 %collective-permute-start.10 = (f32[8,128]{1,0:T(8,128)S(1)}, f32[8,128]{1,0:T(8,128)S(1)}, u32[]{:S(2)}, u32[]{:S(2)}) collective-permute-start(f32[8,128]{1,0:T(8,128)S(1)} %get-tuple-element.42), channel_id=1, source_target_pairs={{0,128},{32,160},{64,192},{96,224},{128,0},{160,32},{192,64},{224,... | collective-permute-start | bytes 12296 | tf_op jit(solution)/shard_map/ppermute | solution.py:31
  28.5 4.8 %collective-permute-start.9 = (f32[8,128]{1,0:T(8,128)S(1)}, f32[8,128]{1,0:T(8,128)S(1)}, u32[]{:S(2)}, u32[]{:S(2)}) collective-permute-start(f32[8,128]{1,0:T(8,128)S(1)} %get-tuple-element.42), channel_id=1, source_target_pairs={{0,192},{32,224},{64,128},{96,160},{128,64},{160,96},{192,0},{224,... | collective-permute-start | bytes 12296 | tf_op jit(solution)/shard_map/ppermute | solution.py:31
  29.6 3.8 %collective-permute-start.8 = (f32[8,128]{1,0:T(8,128)S(1)}, f32[8,128]{1,0:T(8,128)S(1)}, u32[]{:S(2)}, u32[]{:S(2)}) collective-permute-start(f32[8,128]{1,0:T(8,128)S(1)} %get-tuple-element.42), channel_id=1, source_target_pairs={{0,64},{32,96},{64,0},{96,32},{128,192},{160,224},{192,128},{224,1... | collective-permute-start | bytes 12296 | tf_op jit(solution)/shard_map/ppermute | solution.py:31
  33.4 7.6 %collective-permute-start.11 = (f32[8,128]{1,0:T(8,128)S(1)}, f32[8,128]{1,0:T(8,128)S(1)}, u32[]{:S(2)}, u32[]{:S(2)}) collective-permute-start(f32[8,128]{1,0:T(8,128)S(1)} %add_add_fusion), channel_id=1, source_target_pairs={{0,32},{32,0},{64,96},{96,64},{128,160},{160,128},{192,224},{224,1... | collective-permute-start | bytes 12296 | tf_op jit(solution)/shard_map/ppermute | solution.py:31
